TPU v7x, 512 devices: a whole 4x8x8 slice. The times are simulated.
512 devices in a mesh: out: 16 (over y_hi, z), in: 32 (over y_lo, x, core).
Axes of the slice: x: 4, y: 8 (y_hi: 2, y_lo: 4; y = y_hi * 4 + y_lo), z: 8, core: 2. Of those that a mesh axis runs over, the one named last changes fastest.
Arguments:
- tensor: bfloat16 [1024, 1024, 1024], P('out', 'in'), may hold values from -0.01171875 to 0.01171875
- linear: bfloat16 [1024, 1024], P('out', 'in'), may hold values from -0.1875 to 0.1875
- adjoint_end: float32 [128, 1024], P(None, 'in'), may hold values from -6 to 6
- states: bfloat16 [2, 128, 1024], replicated, may hold values from -6 to 6
Outputs:
- adjoint_start: float32 [128, 1024], P(None, 'in')
All inputs are finite; a program needn't handle non-finite values.
Results may differ from a plain program's by a relative error of at most 0.0045.
Values may be sent and summed in bfloat16 or wider, within the bound.
No kernel may reach another device: no remote copies, remote signals or barrier semaphores. Data moves between devices by JAX's collectives and lax.ppermute only.
A program may use at most 64 MiB of HBM per device.

v0:
```python
import jax
import jax.numpy as jnp
from jax import lax
from jax.sharding import PartitionSpec as P

step_size = 0.5


def pieces(tensor, linear, state, full_low):
    rows_block = tensor.shape[0]
    cols_block = tensor.shape[1]
    modes = tensor.shape[2]
    batch = full_low.shape[0]
    lam_rows = lax.dynamic_slice_in_dim(full_low, lax.axis_index("out") * rows_block, rows_block, 1)
    state_cols = lax.dynamic_slice_in_dim(state, lax.axis_index("in") * cols_block, cols_block, 1)
    flat = tensor.reshape(rows_block * cols_block, modes)
    projected = lax.dot_general(
        state, flat, (((1,), (1,)), ((), ())), preferred_element_type=jnp.float32
    )
    projected = projected.reshape(batch, rows_block, cols_block)
    lam_float = lam_rows.astype(jnp.float32)
    first = jnp.einsum("bi,bij->bj", lam_float, projected)
    lin = jnp.dot(lam_rows, linear, preferred_element_type=jnp.float32)
    pair = (lam_float[:, :, None] * state_cols.astype(jnp.float32)[:, None, :]).astype(jnp.bfloat16)
    second = jnp.dot(
        pair.reshape(batch, rows_block * cols_block), flat, preferred_element_type=jnp.float32
    )
    return (lin + first, second)


def per_device(tensor, linear, adjoint_end, states):
    steps_total = states.shape[0]
    lam_own = adjoint_end
    for number in range(steps_total - 1, -1, -1):
        full_low = lax.all_gather(lam_own.astype(jnp.bfloat16), "in", axis=1, tiled=True)
        local, second = pieces(tensor, linear, states[number], full_low)
        second_own = lax.psum_scatter(second, "in", scatter_dimension=1, tiled=True)
        total = lax.psum(local + second_own, "out")
        lam_own = lam_own + step_size * total
    return lam_own


def solution(mesh):
    placed = (P("out", "in", None), P("out", "in"), P(None, "in"), P())
    return jax.shard_map(
        per_device, mesh=mesh, in_specs=placed, out_specs=P(None, "in"), check_vma=False
    )
```

profile of v0, /device:TPU:32, one launch (start us, length us, event | category | flops | bytes accessed | tf_op | source)
XLA Modules:
  0.0 597.5 jit_solution(11177470907793793532)
XLA Ops:
  6.5 0.0 copy-start
  6.5 0.0 reduce-scatter.3.cloned.1.call-start
  6.5 0.7 convert_element_type.38
  7.3 41.3 %all_gather.6 = bf16[128,1024]{0,1:T(8,128)(2,1)S(1)} all-gather(bf16[128,32]{0,1:T(8,128)(2,1)S(1)} %convert_element_type.38), channel_id=1, replica_groups=mesh['out'=16,'in'=32] {'in'}, dimensions={1}, use_global_device_ids=true | all-gather | bytes 270336 | tf_op jit(solution)/shard_map/all_gather | solution.py:35
  48.6 0.0 copy-start.1
  48.6 1.1 fusion.34
  49.7 0.1 bitcast_convert_fusion.1
  49.8 0.1 copy.13
  49.9 8.0 %fusion.10 = f32[128,1024]{0,1:T(8,128)} fusion(bf16[64,32,1024]{2,1,0:T(8,128)(2,1)} %param.4, f32[128,32]{0,1:T(8,128)S(1)} %copy.13, f32[128,64]{0,1:T(8,128)S(1)} %dynamic-slice_convert_fusion.1), kind=kOutput, calls=%fused_computation.9 | convolution fusion | flops 537395200 | bytes 4767744 | tf_op jit(solution)/shard_map/dot_general | solution.py:25
  57.8 0.0 copy-start.2
  57.8 0.0 reduce-scatter.3.cloned.1.call-update
  57.8 0.0 reduce-scatter.5.cloned.1.call-start
  57.9 0.1 bitcast_convert_fusion
  58.0 0.1 copy.16
  58.0 0.0 copy-done.1
  58.0 3.5 fusion.9
  61.5 144.3 %reduce-scatter.3.cloned.1.call-done = f32[128,32]{0,1:T(8,128)} async-done(((f32[128,1024]{0,1:T(8,128)}), f32[128,32]{0,1:T(8,128)}) %reduce-scatter.3.cloned.1.call-update) | async-done | bytes 16400 | tf_op jit(solution)/shard_map/reduce_scatter | solution.py:37
  205.8 0.0 copy-done
  205.8 0.8 fusion.20
  206.7 97.6 %psum.14 = f32[128,32]{0,1:T(8,128)S(1)} all-reduce(f32[128,32]{0,1:T(8,128)S(1)} %fusion.20), channel_id=1, replica_groups=mesh['out'=16,'in'=32] {'out'}, use_global_device_ids=true, to_apply=%region_1.0 | all-reduce | flops 4096 | bytes 32768 | tf_op jit(solution)/shard_map/psum | solution.py:38
  304.3 0.0 copy-done.2
  304.3 38.5 %all_gather.7 = bf16[128,1024]{0,1:T(8,128)(2,1)S(1)} all-gather(bf16[128,32]{0,1:T(8,128)(2,1)S(1)} %fusion.29), channel_id=1, replica_groups=mesh['out'=16,'in'=32] {'in'}, dimensions={1}, use_global_device_ids=true | all-gather | bytes 270336 | tf_op jit(solution)/shard_map/all_gather | solution.py:35
  342.8 7.9 %fusion.13 = f32[128,1024]{0,1:T(8,128)} fusion(bf16[64,32,1024]{2,1,0:T(8,128)(2,1)} %param.4, f32[128,64]{0,1:T(8,128)S(1)} %dynamic-slice_convert_fusion, f32[128,32]{0,1:T(8,128)S(1)} %copy.16), kind=kOutput, calls=%fused_computation.10 | convolution fusion | flops 537395200 | bytes 4767744 | tf_op jit(solution)/shard_map/dot_general | solution.py:25
  350.7 0.0 reduce-scatter.5.cloned.1.call-update
  350.7 6.9 %fusion.16 = f32[128,32]{0,1:T(8,128)S(1)} fusion(bf16[64,32,1024]{2,1,0:T(8,128)(2,1)} %param.4, f32[128,64]{0,1:T(8,128)S(1)} %dynamic-slice_convert_fusion, bf16[2,128,1024]{2,1,0:T(8,128)(2,1)S(1)} %copy-done.1), kind=kOutput, calls=%fused_computation.11 | convolution fusion | flops 537391104 | bytes 4505600 | tf_op jit(solution)/shard_map/dot_general | solution.py:17
  357.6 133.9 %reduce-scatter.5.cloned.1.call-done = f32[128,32]{0,1:T(8,128)} async-done(((f32[128,1024]{0,1:T(8,128)}), f32[128,32]{0,1:T(8,128)}) %reduce-scatter.5.cloned.1.call-update) | async-done | bytes 16400 | tf_op jit(solution)/shard_map/reduce_scatter | solution.py:37
  491.6 0.8 fusion.19
  492.4 97.6 %psum.15 = f32[128,32]{0,1:T(8,128)S(1)} all-reduce(f32[128,32]{0,1:T(8,128)S(1)} %fusion.19), channel_id=1, replica_groups=mesh['out'=16,'in'=32] {'out'}, use_global_device_ids=true, to_apply=%region_3.0 | all-reduce | flops 4096 | bytes 32768 | tf_op jit(solution)/shard_map/psum | solution.py:38
  590.1 0.6 multiply_add_fusion
  (3 shorter events, 0.0 us)
Async XLA Ops:
  6.5 199.3 %copy-start = (bf16[64,32]{0,1:T(8,128)(2,1)S(1)}, bf16[64,32]{0,1:T(8,128)(2,1)}, u32[]{:S(2)}) copy-start(bf16[64,32]{0,1:T(8,128)(2,1)} %param.5) | copy-start | bytes 12292
  6.5 199.3 %reduce-scatter.3.cloned.1.call-start = ((), (), s32[]{:S(2)}) async-start(), calls=%async_computation.2 | async-start | bytes 540672 | tf_op jit(solution)/shard_map/reduce_scatter | solution.py:37
  48.6 9.5 %copy-start.1 = (bf16[2,128,1024]{2,1,0:T(8,128)(2,1)S(1)}, bf16[2,128,1024]{2,1,0:T(8,128)(2,1)}, u32[]{:S(2)}) copy-start(bf16[2,128,1024]{2,1,0:T(8,128)(2,1)} %param.7) | copy-start | bytes 1572868
  57.8 246.5 %copy-start.2 = (f32[128,32]{0,1:T(8,128)S(1)}, f32[128,32]{0,1:T(8,128)}, u32[]{:S(2)}) copy-start(f32[128,32]{0,1:T(8,128)} %param.6) | copy-start | bytes 49156
  57.8 433.7 %reduce-scatter.5.cloned.1.call-start = ((), (), s32[]{:S(2)}) async-start(), calls=%async_computation.3 | async-start | bytes 540672 | tf_op jit(solution)/shard_map/reduce_scatter | solution.py:37
Sparse Core Ops, SparseCore 0:
  58.0 147.8 reduce-scatter.2
  350.8 140.7 reduce-scatter.4
where the time goes:
time: 598 us
  waiting for transfers between devices  278 us (46%)
  blocking collectives  275 us (46%)
  matrix products  28 us (5%)
  between operations  13.4 us (2%)
    reduce_scatter x2, waiting for transfers between devices, per_device(): second_own = lax.psum_scatter(second, 'in', scatter_dimension=1, tiled=True)  278 us
    psum x2, blocking collectives, per_device(): total = lax.psum(local + second_own, 'out')  195 us
    all_gather x2, blocking collectives, per_device(): lax.all_gather(lam_own.astype(jnp.bfloat16), 'in', axis=1, tiled=True)  79.8 us
    dot_general x2, matrix products, pieces(): jnp.dot(pair.reshape(batch, rows_block * cols_block), flat, preferred_ele...  15.9 us
  transfers between devices with their start and end apart: 2, of which 2 were waited for; matrix products, arithmetic and copies ran while one was open for 2% of the time, Pallas kernels for 0%

commit v1 on v0

v1 whole, which is shorter than its diff:
```python
import jax
import jax.numpy as jnp
import numpy as np
from jax import lax
from jax.sharding import Mesh, PartitionSpec as P

step_size = 0.5
AXES = ("yhi", "z", "ylo", "x", "core")
SIZES = (2, 8, 4, 4, 2)
OUT = ("yhi", "z")
IN = ("ylo", "x", "core")
CHIP = ("ylo", "x")


def ring(a, b, n):
    d = abs(a - b) % n
    return min(d, n - d)


def spread_pairs():
    pairs = []
    for o in range(16):
        yhi, z = divmod(o, 8)
        ylo, x = divmod(o, 4)
        hold = [(h, k) for h in range(2) for k in range(8)]
        want = [(a, b) for a in range(4) for b in range(4)]
        cost = np.array(
            [
                [ring(k, z, 8) + ring(h * 4 + ylo, yhi * 4 + a, 8) + ring(x, b, 4) for a, b in want]
                for h, k in hold
            ]
        )
        best = assign(cost)
        for i, j in enumerate(best):
            pairs.append(((hold[i][0] * 8 + hold[i][1]) * 16 + o, o * 16 + want[j][0] * 4 + want[j][1]))
    return pairs


def assign(cost):
    n = len(cost)
    for limit in range(int(cost.max()) + 1):
        owner = [-1] * n

        def place(i, seen):
            for j in range(n):
                if cost[i][j] <= limit and j not in seen:
                    seen.add(j)
                    if owner[j] < 0 or place(owner[j], seen):
                        owner[j] = i
                        return True
            return False

        if all(place(i, set()) for i in range(n)):
            match = [0] * n
            for j, i in enumerate(owner):
                match[i] = j
            return match
    raise ValueError("no matching")


def start_rows(own):
    perm = [(2 * a + c, 2 * b + c) for a, b in spread_pairs() for c in range(2)]
    return lax.ppermute(own, AXES, perm)


def core_half(partial):
    batch = partial.shape[1]
    both = lax.all_gather(partial.astype(jnp.bfloat16), "core")
    both = both.reshape(2, 16, 2, 32, batch)
    mine = lax.dynamic_index_in_dim(both, lax.axis_index("core"), 2, keepdims=False)
    return (mine[0].astype(jnp.float32) + mine[1].astype(jnp.float32)).astype(jnp.bfloat16)


def scatter_sum(pieces, axes):
    got = lax.all_to_all(pieces, axes, 0, 0, tiled=True)
    return jnp.sum(got.astype(jnp.float32), 0)


def spread_sum(piece, axes):
    copies = jnp.broadcast_to(piece.astype(jnp.bfloat16)[None], (16,) + piece.shape)
    got = lax.all_to_all(copies, axes, 0, 0, tiled=True)
    return jnp.sum(got.astype(jnp.float32), 0)


def partial_of(flat, linear, projected, cols, low, slot):
    rows, batch = low.shape
    width = cols.shape[0]
    low_float = low.astype(jnp.float32)
    pair = (low_float[:, None, :] * cols.astype(jnp.float32)[None]).astype(jnp.bfloat16)
    second = lax.dot_general(
        flat, pair.reshape(rows * width, batch), (((0,), (0,)), ((), ())), preferred_element_type=jnp.float32
    )
    first = jnp.sum(low_float[:, None, :] * projected.reshape(rows, width, batch), 0)
    lin = lax.dot_general(linear, low, (((0,), (0,)), ((), ())), preferred_element_type=jnp.float32)
    mine = lax.broadcasted_iota(jnp.int32, (1024 // width, 1, 1), 0) == slot
    return (second.reshape(-1, width, batch) + jnp.where(mine, (first + lin)[None], 0.0)).reshape(-1, batch)


def per_device(tensor, linear, adjoint_end, states):
    rows, width, modes = tensor.shape
    steps, batch = states.shape[:2]
    slot = lax.axis_index(IN)
    flat = tensor.reshape(rows * width, modes)
    own = adjoint_end.T
    lam = start_rows(own)
    projected = lax.dot_general(
        flat, states.reshape(steps * batch, modes), (((1,), (1,)), ((), ())), preferred_element_type=jnp.float32
    )
    total = None
    for number in range(steps - 1, -1, -1):
        low = lax.all_gather(lam.astype(jnp.bfloat16), "core").reshape(rows, batch)
        cols = lax.dynamic_slice_in_dim(states[number], slot * width, width, 1).T
        part = partial_of(
            flat, linear, projected[:, number * batch : (number + 1) * batch], cols, low, slot
        )
        total = part if total is None else total + part
        if number:
            lam = lam + step_size * spread_sum(scatter_sum(core_half(part), OUT), CHIP)
    last = spread_sum(scatter_sum(core_half(total), CHIP), OUT)
    return (own + step_size * last).T


def solution(mesh):
    fine = Mesh(mesh.devices.reshape(SIZES), AXES)
    placed = (P(OUT, IN, None), P(OUT, IN), P(None, IN), P())
    return jax.shard_map(
        per_device, mesh=fine, in_specs=placed, out_specs=P(None, IN), check_vma=False
    )
```

time: 598 us -> 108 us (0.18)
  the two profiles are of different devices: /device:TPU:32 before, /device:TPU:2 now
where the time goes in v1:
time: 108 us; the launch traced here: 107 us
  blocking collectives  64.9 us (60%)
  matrix products  17.8 us (16%)
  starting transfers between devices  10.4 us (10%)
  waiting for transfers between devices  8.61 us (8%)
  local copies, waits for them, and re-layouts  3.23 us (3%)
  other arithmetic  2.16 us (2%)
    all_to_all x2, blocking collectives, scatter_sum(): got = lax.all_to_all(pieces, axes, 0, 0, tiled=True)  40.9 us
    all_to_all x1, blocking collectives, spread_sum(): got = lax.all_to_all(copies, axes, 0, 0, tiled=True)  15.8 us
    dot_general x2, matrix products, partial_of(): lax.dot_general(flat, pair.reshape(rows * width, batch), (((0,), (0,)), (...  13.9 us
    all_to_all x1, waiting for transfers between devices, spread_sum(): got = lax.all_to_all(copies, axes, 0, 0, tiled=True)  7.43 us
    all_to_all x1, starting transfers between devices, spread_sum(): got = lax.all_to_all(copies, axes, 0, 0, tiled=True)  6 us
    ppermute x1, starting transfers between devices, start_rows(): return lax.ppermute(own, AXES, perm)  4.4 us
    all_gather x2, blocking collectives, core_half(): both = lax.all_gather(partial.astype(jnp.bfloat16), 'core')  4.36 us
    all_gather x2, blocking collectives, per_device(): low = lax.all_gather(lam.astype(jnp.bfloat16), 'core').reshape(rows, batch)  3.8 us
  transfers between devices with their start and end apart: 2, of which 2 were waited for; matrix products, arithmetic and copies ran while one was open for 5% of the time, Pallas kernels for 0%

profile of v1, /device:TPU:2, one launch (start us, length us, event | category | flops | bytes accessed | tf_op | source)
XLA Modules:
  0.0 107.2 jit_solution(12274035013023333753)
XLA Ops:
  0.0 4.4 %collective-permute-start = (f32[32,128]{1,0:T(8,128)}, f32[32,128]{1,0:T(8,128)S(1)}, u32[]{:S(2)}, u32[]{:S(2)}) collective-permute-start(f32[32,128]{1,0:T(8,128)} %bitcast.58), channel_id=1, source_target_pairs={{0,18},{1,19},{32,22},{33,23},{64,12},{65,13},{96,4},{97,5},{128,8... | collective-permute-start | bytes 49160 | tf_op jit(solution)/shard_map/ppermute | solution.py:63
  4.4 1.1 fusion.32
  5.5 3.6 %fusion.34 = f32[2048,256]{1,0:T(8,128)S(1)} fusion(bf16[2048,1024]{1,0:T(8,128)(2,1)} %bitcast.59, bf16[256,1024]{1,0:T(8,128)(2,1)} %bitcast.57), kind=kOutput, calls=%fused_computation.37 | convolution fusion | flops 1073741824 | bytes 6815744 | tf_op jit(solution)/shard_map/dot_general | solution.py:106
  9.1 0.1 fusion.31
  9.3 0.1 convert_bitcast_fusion.1
  9.4 0.1 broadcast_in_dim.57
  9.4 0.1 broadcast_in_dim.58
  9.6 1.2 %collective-permute-done = f32[32,128]{1,0:T(8,128)S(1)} collective-permute-done((f32[32,128]{1,0:T(8,128)}, f32[32,128]{1,0:T(8,128)S(1)}, u32[]{:S(2)}, u32[]{:S(2)}) %collective-permute-start) | collective-permute-done | bytes 16416 | tf_op jit(solution)/shard_map/ppermute | solution.py:63
  10.8 1.8 %all-gather = bf16[64,128]{1,0:T(8,128)(2,1)S(1)} all-gather(bf16[32,128]{1,0:T(8,128)(2,1)S(1)} %convert_element_type.88), channel_id=2, replica_groups=mesh['yhi'=2,'z'=8,'ylo'=4,'x'=4,'core'=2] {'core'}, dimensions={0}, use_global_device_ids=true | all-gather | bytes 24576 | tf_op jit(solution)/shard_map/all_gather | solution.py:111
  12.6 0.6 fusion.24
  13.2 0.1 convolution_add_fusion
  13.3 0.1 broadcast_in_dim.60
  13.4 0.2 copy.26
  13.6 6.9 %fusion.33 = (bf16[1024,128]{0,1:T(8,128)(2,1)S(1)}, f32[1024,128]{0,1:T(8,128)S(1)}) fusion(f32[1024,128]{0,1:T(8,128)S(1)} %copy.26, pred[1024]{0:T(1024)(128)(4,1)S(1)} %broadcast_in_dim.58, bf16[64,32,1024]{2,1,0:T(8,128)(2,1)} %param.4, f32[32,128]{1,0:T(8,128)S(1)} %copy.23, f32[64,128]{1,0:T(8,128)S(1)} %convert_element_type.89), kind=kOutput, calls=%fused_computation.36 | convolution fusion | flops 537788416 | bytes 5555200 | tf_op jit(solution)/shard_map/dot_general | solution.py:90
  20.5 2.2 %all-gather.1 = bf16[2048,128]{0,1:T(8,128)(2,1)S(1)} all-gather(bf16[1024,128]{0,1:T(8,128)(2,1)S(1)} %get-tuple-element.9), channel_id=3, replica_groups=mesh['yhi'=2,'z'=8,'ylo'=4,'x'=4,'core'=2] {'core'}, dimensions={0}, use_global_device_ids=true | all-gather | bytes 786432 | tf_op jit(solution)/shard_map/all_gather | solution.py:68
  22.7 0.3 copy.27
  23.1 29.1 %all_to_all.20 = bf16[16,32,128]{2,1,0:T(8,128)(2,1)S(1)} all-to-all(bf16[16,32,128]{2,1,0:T(8,128)(2,1)S(1)} %fusion.29), channel_id=1, replica_groups=mesh['yhi'=2,'z'=8,'ylo'=4,'x'=4,'core'=2] {'yhi','z'}, dimensions={0} | all-to-all | bytes 262144 | tf_op jit(solution)/shard_map/all_to_all | solution.py:75
  52.2 0.7 broadcast_in_dim.63
  52.9 6.0 %all-to-all-start.1 = ((bf16[16,32,128]{2,1,0:T(8,128)(2,1)}), bf16[16,32,128]{2,1,0:T(8,128)(2,1)S(1)}, u32[]{:S(2)}, u32[]{:S(2)}) async-start(bf16[16,32,128]{2,1,0:T(8,128)(2,1)} %broadcast_in_dim.63), calls=%async_computation.1 | async-start | bytes 262144 | tf_op jit(solution)/shard_map/all_to_all | solution.py:81
  58.9 0.1 convert_bitcast_fusion
  59.0 7.4 %all-to-all-done.1 = bf16[16,32,128]{2,1,0:T(8,128)(2,1)S(1)} async-done(((bf16[16,32,128]{2,1,0:T(8,128)(2,1)}), bf16[16,32,128]{2,1,0:T(8,128)(2,1)S(1)}, u32[]{:S(2)}, u32[]{:S(2)}) %all-to-all-start.1) | async-done | bytes 131104 | tf_op jit(solution)/shard_map/all_to_all | solution.py:81
  66.5 2.0 %all-gather.2 = bf16[64,128]{1,0:T(8,128)(2,1)S(1)} all-gather(bf16[32,128]{1,0:T(8,128)(2,1)S(1)} %add_convert_fusion.2), channel_id=4, replica_groups=mesh['yhi'=2,'z'=8,'ylo'=4,'x'=4,'core'=2] {'core'}, dimensions={0}, use_global_device_ids=true | all-gather | bytes 24576 | tf_op jit(solution)/shard_map/all_gather | solution.py:111
  68.5 0.6 fusion.23
  69.1 0.1 fusion.22
  69.2 0.1 broadcast_in_dim.64
  69.3 0.2 copy.31
  69.5 6.9 %fusion.19 = bf16[1024,128]{0,1:T(8,128)(2,1)S(1)} fusion(f32[1024,128]{0,1:T(8,128)S(1)} %get-tuple-element.10, bf16[64,32,1024]{2,1,0:T(8,128)(2,1)} %param.4, f32[1024,128]{0,1:T(8,128)S(1)} %copy.31, f32[32,128]{1,0:T(8,128)S(1)} %copy.28, f32[64,128]{1,0:T(8,128)S(1)} %convert_element_type.101, pred[1024]{0:T(1024)(128)(4,1)S(1)} %broadcast_in_dim.58), kind=kOutput, calls=%fused_computation.9 | convolution fusion | flops 537919488 | bytes 5555200 | tf_op jit(solution)/shard_map/dot_general | solution.py:90
  76.4 2.2 %all-gather.3 = bf16[2048,128]{0,1:T(8,128)(2,1)S(1)} all-gather(bf16[1024,128]{0,1:T(8,128)(2,1)S(1)} %fusion.19), channel_id=5, replica_groups=mesh['yhi'=2,'z'=8,'ylo'=4,'x'=4,'core'=2] {'core'}, dimensions={0}, use_global_device_ids=true | all-gather | bytes 786432 | tf_op jit(solution)/shard_map/all_gather | solution.py:68
  78.6 0.3 copy.32
  79.0 11.8 %all_to_all.21 = bf16[16,32,128]{2,1,0:T(8,128)(2,1)S(1)} all-to-all(bf16[16,32,128]{2,1,0:T(8,128)(2,1)S(1)} %fusion.30), channel_id=1, replica_groups=mesh['yhi'=2,'z'=8,'ylo'=4,'x'=4,'core'=2] {'ylo','x'}, dimensions={0} | all-to-all | bytes 262144 | tf_op jit(solution)/shard_map/all_to_all | solution.py:75
  90.8 15.8 %all_to_all.22 = bf16[16,32,128]{2,1,0:T(8,128)(2,1)S(1)} all-to-all(bf16[16,32,128]{2,1,0:T(8,128)(2,1)S(1)} %broadcast_in_dim.66), channel_id=1, replica_groups=mesh['yhi'=2,'z'=8,'ylo'=4,'x'=4,'core'=2] {'yhi','z'}, dimensions={0} | all-to-all | bytes 262144 | tf_op jit(solution)/shard_map/all_to_all | solution.py:81
  106.6 0.6 bitcast_add_fusion
  (18 shorter events, 0.4 us)
Async XLA Ops:
  0.0 13.2 %copy-start = (bf16[64,32]{0,1:T(8,128)(2,1)S(1)}, bf16[64,32]{0,1:T(8,128)(2,1)}, u32[]{:S(2)}) copy-start(bf16[64,32]{0,1:T(8,128)(2,1)} %param.5) | copy-start | bytes 12292
  0.0 10.8 %collective-permute-start = (f32[32,128]{1,0:T(8,128)}, f32[32,128]{1,0:T(8,128)S(1)}, u32[]{:S(2)}, u32[]{:S(2)}) collective-permute-start(f32[32,128]{1,0:T(8,128)} %bitcast.58), channel_id=1, source_target_pairs={{0,18},{1,19},{32,22},{33,23},{64,12},{65,13},{96,4},{97,5},{128,8... | collective-permute-start | bytes 49160 | tf_op jit(solution)/shard_map/ppermute | solution.py:63
  52.9 13.6 %all-to-all-start.1 = ((bf16[16,32,128]{2,1,0:T(8,128)(2,1)}), bf16[16,32,128]{2,1,0:T(8,128)(2,1)S(1)}, u32[]{:S(2)}, u32[]{:S(2)}) async-start(bf16[16,32,128]{2,1,0:T(8,128)(2,1)} %broadcast_in_dim.63), calls=%async_computation.1 | async-start | bytes 262144 | tf_op jit(solution)/shard_map/all_to_all | solution.py:81
  69.5 37.1 %copy-start.1 = (f32[128,32]{0,1:T(8,128)S(1)}, f32[128,32]{0,1:T(8,128)}, u32[]{:S(2)}) copy-start(f32[128,32]{0,1:T(8,128)} %param.6) | copy-start | bytes 49156

commit v2 on v1

v2 whole, which is shorter than its diff:
```python
import functools

import jax
import jax.numpy as jnp
import numpy as np
from jax import lax
from jax.experimental import pallas as pl
from jax.experimental.pallas import tpu as pltpu
from jax.sharding import Mesh, PartitionSpec as P

step_size = 0.5
VMEM = pl.BlockSpec(memory_space=pltpu.VMEM)
SMEM = pl.BlockSpec(memory_space=pltpu.SMEM)
LIMIT = 16 * 1024 * 1024
AXES = ("yhi", "z", "ylo", "x", "core")
SIZES = (2, 8, 4, 4, 2)
OUT = ("yhi", "z")
IN = ("ylo", "x", "core")
CHIP = ("ylo", "x")
PLANE = ("yhi", "ylo", "x")
R1 = "B"
R0 = "A"


def ring(a, b, n):
    d = abs(a - b) % n
    return min(d, n - d)


def spread_pairs():
    pairs = []
    for o in range(16):
        yhi, z = divmod(o, 8)
        ylo, x = divmod(o, 4)
        hold = [(h, k) for h in range(2) for k in range(8)]
        want = [(a, b) for a in range(4) for b in range(4)]
        cost = np.array(
            [
                [ring(k, z, 8) + ring(h * 4 + ylo, yhi * 4 + a, 8) + ring(x, b, 4) for a, b in want]
                for h, k in hold
            ]
        )
        best = assign(cost)
        for i, j in enumerate(best):
            pairs.append(((hold[i][0] * 8 + hold[i][1]) * 16 + o, o * 16 + want[j][0] * 4 + want[j][1]))
    return pairs


def assign(cost):
    n = len(cost)
    for limit in range(int(cost.max()) + 1):
        owner = [-1] * n

        def place(i, seen):
            for j in range(n):
                if cost[i][j] <= limit and j not in seen:
                    seen.add(j)
                    if owner[j] < 0 or place(owner[j], seen):
                        owner[j] = i
                        return True
            return False

        if all(place(i, set()) for i in range(n)):
            match = [0] * n
            for j, i in enumerate(owner):
                match[i] = j
            return match
    raise ValueError("no matching")


def start_rows(own):
    perm = [(2 * a + c, 2 * b + c) for a, b in spread_pairs() for c in range(2)]
    return lax.ppermute(own, AXES, perm)


def core_half(partial):
    both = lax.all_gather(partial, "core")
    mine = lax.dynamic_index_in_dim(both, lax.axis_index("core"), 1, keepdims=False)
    return (mine[0].astype(jnp.float32) + mine[1].astype(jnp.float32)).astype(jnp.bfloat16)


def exchange(pieces, axes):
    return lax.all_to_all(pieces, axes, 0, 0, tiled=True)


def total_of(got):
    return jnp.sum(got.astype(jnp.float32), 0)


def fold_kernel(got_ref, copies_ref):
    count, groups = got_ref.shape[:2]
    for g in range(groups):
        total = got_ref[0, g].astype(jnp.float32)
        for k in range(1, count):
            total = total + got_ref[k, g].astype(jnp.float32)
        total = total.astype(jnp.bfloat16)
        for m in range(copies_ref.shape[1]):
            copies_ref[g, m] = total


def fold(got, copies):
    groups, width, batch = got.shape[1:]
    out = pl.pallas_call(
        fold_kernel,
        out_shape=jax.ShapeDtypeStruct((groups, copies, width, batch), jnp.bfloat16),
        in_specs=[VMEM],
        out_specs=VMEM,
        compiler_params=pltpu.CompilerParams(vmem_limit_bytes=LIMIT),
        name="fold",
    )(got)
    return out.reshape(groups * copies, width, batch)


def to_out_blocks(half):
    if R1 == "A":
        return total_of(exchange(fold(exchange(half, OUT)[:, None], 16), CHIP))
    two = exchange(half.reshape((8, 2) + half.shape[1:]), "z")
    return total_of(exchange(fold(two, 16), PLANE))


def to_in_blocks(half):
    if R0 == "A":
        return total_of(exchange(fold(exchange(half, CHIP)[:, None], 16), OUT))
    both = jnp.broadcast_to(half[None], (2,) + half.shape).reshape((32,) + half.shape[1:])
    return total_of(exchange(fold(exchange(both, PLANE)[:, None], 8), "z"))


CHUNKS = 8

def load_kernel(slot_ref, tensor_ref, states_ref, kept_ref, projected_ref, cols_ref, sems):
    height = kept_ref.shape[0] // CHUNKS
    loads = []
    for c in range(CHUNKS):
        rows = pl.ds(c * height, height)
        loads.append(pltpu.make_async_copy(tensor_ref.at[rows], kept_ref.at[rows], sems.at[c]))
        loads[-1].start()
    states = states_ref[...]
    shape = (cols_ref.shape[0], states.shape[1])
    wanted = lax.broadcasted_iota(jnp.int32, shape, 0) + slot_ref[0] * shape[0]
    pick = (lax.broadcasted_iota(jnp.int32, shape, 1) == wanted).astype(jnp.bfloat16)
    along = (((1,), (1,)), ((), ()))
    cols_ref[...] = lax.dot_general(pick, states, along, preferred_element_type=jnp.float32)
    for c in range(CHUNKS):
        loads[c].wait()
        rows = slice(c * height, (c + 1) * height)
        projected_ref[rows, :] = lax.dot_general(
            kept_ref[rows, :], states, along, preferred_element_type=jnp.float32
        )


def load(flat, states, slot, width):
    height, modes = flat.shape
    count = states.shape[0]
    return pl.pallas_call(
        load_kernel,
        out_shape=(
            jax.ShapeDtypeStruct(flat.shape, flat.dtype),
            jax.ShapeDtypeStruct((height, count), jnp.float32),
            jax.ShapeDtypeStruct((width, count), jnp.float32),
        ),
        in_specs=[SMEM, pl.BlockSpec(memory_space=pl.ANY), VMEM],
        out_specs=(VMEM, VMEM, VMEM),
        scratch_shapes=[pltpu.SemaphoreType.DMA((CHUNKS,))],
        compiler_params=pltpu.CompilerParams(vmem_limit_bytes=LIMIT),
        name="load",
    )(slot, flat, states)


def step_kernel(has_prev, keep_total, number, order, *refs):
    slot_ref, low_ref, cols_ref, projected_ref, linear_ref, tensor_ref = refs[:6]
    refs = refs[6:]
    if has_prev:
        prev_ref, refs = refs[0], refs[1:]
    send_ref, refs = refs[0], refs[1:]
    if keep_total:
        total_ref, refs = refs[0], refs[1:]
    (pair_ref,) = refs
    rows, batch = low_ref.shape
    width = cols_ref.shape[0]
    mine = slice(number * batch, (number + 1) * batch)
    low = low_ref[...]
    low_float = low.astype(jnp.float32)
    cols = cols_ref[:, mine]
    first = jnp.dot(linear_ref[...], low, preferred_element_type=jnp.float32)
    some = 128 // width
    for c in range(rows // some):
        part = low_float[c * some : (c + 1) * some, :]
        spread = jnp.broadcast_to(part[:, None, :], (some, width, batch))
        here = slice(c * 128, (c + 1) * 128)
        pair = (spread * cols[None]).reshape(128, batch)
        pair_ref[:, here] = pair.T.astype(jnp.bfloat16)
        first = first + jnp.sum(spread * projected_ref[here, mine].reshape(some, width, batch), 0)
    slot = slot_ref[0]
    modes = tensor_ref.shape[1]
    each = 256
    pair = pair_ref[...]
    for n in range(modes // each):
        second = jnp.dot(
            pair, tensor_ref[:, n * each : (n + 1) * each], preferred_element_type=jnp.float32
        ).T
        for k in range(each // width):
            block, half = divmod(n * (each // width) + k, 2)
            piece = second[k * width : (k + 1) * width, :]
            piece = piece + jnp.where(slot == 2 * block + half, first, 0.0)
            if has_prev:
                piece = piece + prev_ref[half, block]
            if keep_total:
                total_ref[half, block] = piece
            send_ref[half, order[block]] = piece.astype(jnp.bfloat16)


def step(flat, linear_t, projected, number, cols, low, slot, prev, keep_total, order):
    modes = flat.shape[1]
    width, batch = cols.shape[0], low.shape[1]
    full = (2, modes // (2 * width), width, batch)
    args = [slot, low, cols, projected, linear_t, flat]
    if prev is not None:
        args.append(prev)
    shapes = [jax.ShapeDtypeStruct(full, jnp.bfloat16)]
    if keep_total:
        shapes.append(jax.ShapeDtypeStruct(full, jnp.float32))
    return pl.pallas_call(
        functools.partial(step_kernel, prev is not None, keep_total, number, tuple(order)),
        out_shape=shapes,
        in_specs=[SMEM] + [VMEM] * (len(args) - 1),
        out_specs=[VMEM] * len(shapes),
        scratch_shapes=[pltpu.VMEM((batch, flat.shape[0]), jnp.bfloat16)],
        compiler_params=pltpu.CompilerParams(vmem_limit_bytes=LIMIT),
        name="step",
    )(*args)


def per_device(tensor, linear, adjoint_end, states):
    rows, width, modes = tensor.shape
    steps, batch = states.shape[:2]
    slot = jnp.reshape(lax.axis_index(IN), (1,)).astype(jnp.int32)
    own = adjoint_end.T
    lam = start_rows(own)
    flat, projected, cols = load(
        tensor.reshape(rows * width, modes), states.reshape(steps * batch, modes), slot, width
    )
    order = range(16) if R1 == "A" else [b % 8 * 2 + b // 8 for b in range(16)]
    total = None
    for number in range(steps - 1, -1, -1):
        low = lax.all_gather(lam.astype(jnp.bfloat16), "core").reshape(rows, batch)
        send, *rest = step(
            flat, linear.T, projected, number, cols, low, slot, total, number > 0, order if number else range(16)
        )
        half = core_half(send)
        if number:
            total = rest[0]
            lam = lam + step_size * to_out_blocks(half)
    return (own + step_size * to_in_blocks(half)).T


def solution(mesh):
    fine = Mesh(mesh.devices.reshape(SIZES), AXES)
    placed = (P(OUT, IN, None), P(OUT, IN), P(None, IN), P())
    return jax.shard_map(
        per_device, mesh=fine, in_specs=placed, out_specs=P(None, IN), check_vma=False
    )
```

time: 108 us -> 93.1 us (0.86)
  matrix products: 17.8 us -> 0 us
  blocking collectives: 64.9 us -> 77.6 us
  waiting for transfers between devices: 8.61 us -> 0.01 us
  Pallas kernels: 0 us -> 6.54 us
  starting transfers between devices: 10.4 us -> 4.4 us
  other arithmetic: 2.16 us -> 0.77 us
    dot_general x5 -> x0, matrix products: 17.8 us -> none  [the longest x2 13.9 us: partial_of(): lax.dot_general(flat, pair.reshape(rows * width, batch), (((0,), (0,)), (...]
    all_to_all x3 -> x4, blocking collectives: 56.7 us -> 69.6 us  [exchange(): return lax.all_to_all(pieces, axes, 0, 0, tiled=True)]
    all_to_all x1 -> x0, waiting for transfers between devices: 7.43 us -> none  [spread_sum(): got = lax.all_to_all(copies, axes, 0, 0, tiled=True)]
    pallas_call x0 -> x5, Pallas kernels: none -> 6.54 us  [the longest x1 4.24 us: load(): pl.pallas_call(load_kernel, out_shape=(jax.ShapeDtypeStruct(flat.shape, f...]
    all_to_all x1 -> x0, starting transfers between devices: 6 us -> none  [spread_sum(): got = lax.all_to_all(copies, axes, 0, 0, tiled=True)]
    unnamed x4 -> x8, local copies, waits for them, and re-layouts: 0.01 us -> 3.23 us
    broadcast_in_dim x8 -> x0, local copies, waits for them, and re-layouts: 1.35 us -> none  [the longest x2 0.68 us: spread_sum(): jnp.broadcast_to(piece.astype(jnp.bfloat16)[None], (16,) + piece.shape)]
    slice x2 -> x0, local copies, waits for them, and re-layouts: 1.2 us -> none  [the longest x1 1.07 us: per_device(): cols = lax.dynamic_slice_in_dim(states[number], slot * width, width, 1).T]
  transfers between devices with their start and end apart: 2 -> 1, of which waited for: 2 -> 0; matrix products, arithmetic and copies ran while one was open for 5% -> 0% of each run, Pallas kernels for 0% -> 5%
where the time goes in v2:
time: 93.1 us; the launch traced here: 92.7 us
  blocking collectives  77.6 us (83%)
  Pallas kernels  6.54 us (7%)
  starting transfers between devices  4.4 us (5%)
  local copies, waits for them, and re-layouts  3.23 us (3%)
    all_to_all x4, blocking collectives, exchange(): return lax.all_to_all(pieces, axes, 0, 0, tiled=True)  69.6 us
    ppermute x1, starting transfers between devices, start_rows(): return lax.ppermute(own, AXES, perm)  4.4 us
    all_gather x2, blocking collectives, core_half(): both = lax.all_gather(partial, 'core')  4.36 us
    pallas_call x1, Pallas kernels, load(): pl.pallas_call(load_kernel, out_shape=(jax.ShapeDtypeStruct(flat.shape, f...  4.24 us
    all_gather x2, blocking collectives, per_device(): low = lax.all_gather(lam.astype(jnp.bfloat16), 'core').reshape(rows, batch)  3.64 us
    unnamed x8, local copies, waits for them, and re-layouts  3.23 us
    pallas_call x2, Pallas kernels, step(): pl.pallas_call(functools.partial(step_kernel, prev is not None, keep_tota...  2.25 us
  transfers between devices with their start and end apart: 1, of which 0 were waited for; matrix products, arithmetic and copies ran while one was open for 0% of the time, Pallas kernels for 5%

profile of v2, /device:TPU:2, one launch (start us, length us, event | category | flops | bytes accessed | tf_op | source)
XLA Modules:
  0.0 92.7 jit_solution(14885657966152085713)
XLA Ops:
  0.0 0.0 copy-start.2
  0.0 4.4 %collective-permute-start = (f32[32,128]{1,0:T(8,128)}, f32[32,128]{1,0:T(8,128)S(1)}, u32[]{:S(2)}, u32[]{:S(2)}) collective-permute-start(f32[32,128]{1,0:T(8,128)} %bitcast.25), channel_id=1, source_target_pairs={{0,18},{1,19},{32,22},{33,23},{64,12},{65,13},{96,4},{97,5},{128,8... | collective-permute-start | bytes 49160 | tf_op jit(solution)/shard_map/ppermute | solution.py:73
  4.4 0.0 copy-start
  4.4 2.2 %copy-done = bf16[64,32,1024]{2,1,0:T(8,128)(2,1)S(1)} copy-done((bf16[64,32,1024]{2,1,0:T(8,128)(2,1)S(1)}, bf16[64,32,1024]{2,1,0:T(8,128)(2,1)}, u32[]{:S(2)}) %copy-start) | copy-done | bytes 4194328
  6.6 0.0 copy-start.1
  6.6 1.0 %copy-done.1 = bf16[2,128,1024]{2,1,0:T(8,128)(2,1)S(1)} copy-done((bf16[2,128,1024]{2,1,0:T(8,128)(2,1)S(1)}, bf16[2,128,1024]{2,1,0:T(8,128)(2,1)}, u32[]{:S(2)}) %copy-start.1) | copy-done | bytes 524312
  7.7 4.2 %load.1 = (bf16[2048,1024]{1,0:T(8,128)(2,1)S(1)}, f32[2048,256]{1,0:T(8,128)S(1)}, f32[32,256]{1,0:T(8,128)S(1)}) custom-call(s32[1]{0:T(128)} %bitcast.slot_ref.refs_0_, bf16[2048,1024]{1,0:T(8,128)(2,1)S(1)} %bitcast.15, bf16[256,1024]{1,0:T(8,128)(2,1)S(1)} %bitcast.17), custom_call_target="tpu_custom_call" | custom-call | tf_op jit(solution)/shard_map/load/pallas_call | solution.py:154
  11.9 0.0 collective-permute-done
  11.9 1.8 %all-gather.refs_1_ = bf16[64,128]{1,0:T(8,128)(2,1)S(1)} all-gather(bf16[32,128]{1,0:T(8,128)(2,1)S(1)} %convert_element_type.43), channel_id=2, replica_groups=mesh['yhi'=2,'z'=8,'ylo'=4,'x'=4,'core'=2] {'core'}, dimensions={0}, use_global_device_ids=true | all-gather | bytes 24576 | tf_op jit(solution)/shard_map/all_gather | solution.py:245
  13.7 0.0 copy-done.2
  13.7 1.1 %step.2 = (bf16[2,16,32,128]{3,2,1,0:T(8,128)(2,1)S(1)}, f32[2,16,32,128]{3,2,1,0:T(8,128)S(1)}) custom-call(s32[1]{0:T(128)} %bitcast.slot_ref.refs_0_, bf16[64,128]{1,0:T(8,128)(2,1)S(1)} %all-gather.refs_1_, f32[32,256]{1,0:T(8,128)S(1)} %get-tuple-element.10.refs_2_, f32[2048,256]{1,0:T(8,128)S(1)} %get-tuple-element.11.refs_3_, ...), custom_call_target="tpu_custom_call" | custom-call | tf_op jit(solution)/shard_map/step/pallas_call | solution.py:222
  14.9 2.2 %all-gather.1 = bf16[4,16,32,128]{3,2,1,0:T(8,128)(2,1)S(1)} all-gather(bf16[2,16,32,128]{3,2,1,0:T(8,128)(2,1)S(1)} %get-tuple-element.13), channel_id=3, replica_groups=mesh['yhi'=2,'z'=8,'ylo'=4,'x'=4,'core'=2] {'core'}, dimensions={0}, use_global_device_ids=true | all-gather | bytes 786432 | tf_op jit(solution)/shard_map/all_gather | solution.py:77
  17.1 20.0 %all_to_all.20.got_ref = bf16[8,2,32,128]{3,2,1,0:T(8,128)(2,1)S(1)} all-to-all(bf16[8,2,32,128]{3,2,1,0:T(8,128)(2,1)S(1)} %bitcast.24), channel_id=1, replica_groups=mesh['yhi'=2,'z'=8,'ylo'=4,'x'=4,'core'=2] {'z'}, dimensions={0} | all-to-all | bytes 262144 | tf_op jit(solution)/shard_map/all_to_all | solution.py:83
  37.1 20.4 %all_to_all.21 = bf16[32,32,128]{2,1,0:T(8,128)(2,1)S(1)} all-to-all(bf16[32,32,128]{2,1,0:T(8,128)(2,1)S(1)} %bitcast.16), channel_id=1, replica_groups=mesh['yhi'=2,'z'=8,'ylo'=4,'x'=4,'core'=2] {'yhi','ylo','x'}, dimensions={0} | all-to-all | bytes 524288 | tf_op jit(solution)/shard_map/all_to_all | solution.py:83
  57.5 1.8 %all-gather.2.refs_1_ = bf16[64,128]{1,0:T(8,128)(2,1)S(1)} all-gather(bf16[32,128]{1,0:T(8,128)(2,1)S(1)} %add_convert_fusion.2), channel_id=4, replica_groups=mesh['yhi'=2,'z'=8,'ylo'=4,'x'=4,'core'=2] {'core'}, dimensions={0}, use_global_device_ids=true | all-gather | bytes 24576 | tf_op jit(solution)/shard_map/all_gather | solution.py:245
  59.4 0.0 copy-start.3
  59.4 1.1 %step.3 = bf16[2,16,32,128]{3,2,1,0:T(8,128)(2,1)S(1)} custom-call(s32[1]{0:T(128)} %bitcast.slot_ref.refs_0_, bf16[64,128]{1,0:T(8,128)(2,1)S(1)} %all-gather.2.refs_1_, f32[32,256]{1,0:T(8,128)S(1)} %get-tuple-element.10.refs_2_, f32[2048,256]{1,0:T(8,128)S(1)} %get-tuple-element.11.refs_3_, bf16[32,64]{1,0:T(8,128)(2,1)S(1)} %bitcast.21, ...), custom_call_target="tpu_custom_call" | custom-call | tf_op jit(solution)/shard_map/step/pallas_call | solution.py:222
  60.5 2.2 %all-gather.3 = bf16[4,16,32,128]{3,2,1,0:T(8,128)(2,1)S(1)} all-gather(bf16[2,16,32,128]{3,2,1,0:T(8,128)(2,1)S(1)} %step.3), channel_id=5, replica_groups=mesh['yhi'=2,'z'=8,'ylo'=4,'x'=4,'core'=2] {'core'}, dimensions={0}, use_global_device_ids=true | all-gather | bytes 786432 | tf_op jit(solution)/shard_map/all_gather | solution.py:77
  62.7 12.4 %all_to_all.22 = bf16[16,32,128]{2,1,0:T(8,128)(2,1)S(1)} all-to-all(bf16[16,32,128]{2,1,0:T(8,128)(2,1)S(1)} %fusion), channel_id=1, replica_groups=mesh['yhi'=2,'z'=8,'ylo'=4,'x'=4,'core'=2] {'ylo','x'}, dimensions={0} | all-to-all | bytes 262144 | tf_op jit(solution)/shard_map/all_to_all | solution.py:83
  75.2 16.8 %all_to_all.23 = bf16[16,32,128]{2,1,0:T(8,128)(2,1)S(1)} all-to-all(bf16[16,32,128]{2,1,0:T(8,128)(2,1)S(1)} %bitcast.19), channel_id=1, replica_groups=mesh['yhi'=2,'z'=8,'ylo'=4,'x'=4,'core'=2] {'yhi','z'}, dimensions={0} | all-to-all | bytes 262144 | tf_op jit(solution)/shard_map/all_to_all | solution.py:83
  92.0 0.0 copy-done.3
  92.1 0.6 bitcast_add_fusion
  (8 shorter events, 0.2 us)
Async XLA Ops:
  0.0 13.7 %copy-start.2 = (bf16[64,32]{0,1:T(8,128)(2,1)S(1)}, bf16[64,32]{0,1:T(8,128)(2,1)}, u32[]{:S(2)}) copy-start(bf16[64,32]{0,1:T(8,128)(2,1)} %param.5) | copy-start | bytes 12292
  0.0 11.9 %collective-permute-start = (f32[32,128]{1,0:T(8,128)}, f32[32,128]{1,0:T(8,128)S(1)}, u32[]{:S(2)}, u32[]{:S(2)}) collective-permute-start(f32[32,128]{1,0:T(8,128)} %bitcast.25), channel_id=1, source_target_pairs={{0,18},{1,19},{32,22},{33,23},{64,12},{65,13},{96,4},{97,5},{128,8... | collective-permute-start | bytes 49160 | tf_op jit(solution)/shard_map/ppermute | solution.py:73
  4.4 2.2 %copy-start = (bf16[64,32,1024]{2,1,0:T(8,128)(2,1)S(1)}, bf16[64,32,1024]{2,1,0:T(8,128)(2,1)}, u32[]{:S(2)}) copy-start(bf16[64,32,1024]{2,1,0:T(8,128)(2,1)} %param.4) | copy-start | bytes 12582916
  6.6 1.0 %copy-start.1 = (bf16[2,128,1024]{2,1,0:T(8,128)(2,1)S(1)}, bf16[2,128,1024]{2,1,0:T(8,128)(2,1)}, u32[]{:S(2)}) copy-start(bf16[2,128,1024]{2,1,0:T(8,128)(2,1)} %param.7) | copy-start | bytes 1572868
  59.4 32.7 %copy-start.3 = (f32[128,32]{0,1:T(8,128)S(1)}, f32[128,32]{0,1:T(8,128)}, u32[]{:S(2)}) copy-start(f32[128,32]{0,1:T(8,128)} %param.6) | copy-start | bytes 49156

commit v3 on v2

--- a/solution.py
+++ b/solution.py
@@ -10,6 +10,7 @@
 
 step_size = 0.5
 VMEM = pl.BlockSpec(memory_space=pltpu.VMEM)
+HBM = pl.BlockSpec(memory_space=pltpu.HBM)
 SMEM = pl.BlockSpec(memory_space=pltpu.SMEM)
 LIMIT = 16 * 1024 * 1024
 AXES = ("yhi", "z", "ylo", "x", "core")
@@ -52,7 +53,7 @@
         owner = [-1] * n
 
         def place(i, seen):
-            for j in range(n):
+            for j in sorted(range(n), key=lambda k: cost[i][k]):
                 if cost[i][j] <= limit and j not in seen:
                     seen.add(j)
                     if owner[j] < 0 or place(owner[j], seen):
@@ -69,14 +70,22 @@
 
 
 def start_rows(own):
-    perm = [(2 * a + c, 2 * b + c) for a, b in spread_pairs() for c in range(2)]
-    return lax.ppermute(own, AXES, perm)
-
-
-def core_half(partial):
-    both = lax.all_gather(partial, "core")
-    mine = lax.dynamic_index_in_dim(both, lax.axis_index("core"), 1, keepdims=False)
-    return (mine[0].astype(jnp.float32) + mine[1].astype(jnp.float32)).astype(jnp.bfloat16)
+    pairs = spread_pairs()
+    same = [(2 * a + c, 2 * b + c) for a, b in pairs for c in range(2)]
+    cross = [(2 * a + c, 2 * b + 1 - c) for a, b in pairs for c in range(2)]
+    other = lax.ppermute(own.astype(jnp.bfloat16), AXES, cross)
+    return lax.ppermute(own, AXES, same), other
+
+
+def in_order(mine, other):
+    first = lax.axis_index("core") == 0
+    return jnp.concatenate([jnp.where(first, mine, other), jnp.where(first, other, mine)], 0)
+
+
+def core_half(keep, send):
+    both = lax.all_gather(send, "core")
+    got = lax.dynamic_index_in_dim(both, 1 - lax.axis_index("core"), 0, keepdims=False)
+    return (keep + got.astype(jnp.float32)).astype(jnp.bfloat16)
 
 
 def exchange(pieces, axes):
@@ -127,13 +136,16 @@
 
 CHUNKS = 8
 
-def load_kernel(slot_ref, tensor_ref, states_ref, kept_ref, projected_ref, cols_ref, sems):
+def load_kernel(slot_ref, tensor_ref, source_ref, kept_ref, projected_ref, cols_ref, states_ref, sems):
     height = kept_ref.shape[0] // CHUNKS
+    first = pltpu.make_async_copy(source_ref, states_ref, sems.at[CHUNKS])
+    first.start()
     loads = []
     for c in range(CHUNKS):
         rows = pl.ds(c * height, height)
         loads.append(pltpu.make_async_copy(tensor_ref.at[rows], kept_ref.at[rows], sems.at[c]))
         loads[-1].start()
+    first.wait()
     states = states_ref[...]
     shape = (cols_ref.shape[0], states.shape[1])
     wanted = lax.broadcasted_iota(jnp.int32, shape, 0) + slot_ref[0] * shape[0]
@@ -158,9 +170,9 @@
             jax.ShapeDtypeStruct((height, count), jnp.float32),
             jax.ShapeDtypeStruct((width, count), jnp.float32),
         ),
-        in_specs=[SMEM, pl.BlockSpec(memory_space=pl.ANY), VMEM],
+        in_specs=[SMEM, HBM, HBM],
         out_specs=(VMEM, VMEM, VMEM),
-        scratch_shapes=[pltpu.SemaphoreType.DMA((CHUNKS,))],
+        scratch_shapes=[pltpu.VMEM(states.shape, states.dtype), pltpu.SemaphoreType.DMA((CHUNKS + 1,))],
         compiler_params=pltpu.CompilerParams(vmem_limit_bytes=LIMIT),
         name="load",
     )(slot, flat, states)
@@ -171,7 +183,7 @@
     refs = refs[6:]
     if has_prev:
         prev_ref, refs = refs[0], refs[1:]
-    send_ref, refs = refs[0], refs[1:]
+    keep_ref, send_ref, refs = refs[0], refs[1], refs[2:]
     if keep_total:
         total_ref, refs = refs[0], refs[1:]
     (pair_ref,) = refs
@@ -198,15 +210,20 @@
         second = jnp.dot(
             pair, tensor_ref[:, n * each : (n + 1) * each], preferred_element_type=jnp.float32
         ).T
-        for k in range(each // width):
-            block, half = divmod(n * (each // width) + k, 2)
-            piece = second[k * width : (k + 1) * width, :]
-            piece = piece + jnp.where(slot == 2 * block + half, first, 0.0)
-            if has_prev:
-                piece = piece + prev_ref[half, block]
-            if keep_total:
-                total_ref[half, block] = piece
-            send_ref[half, order[block]] = piece.astype(jnp.bfloat16)
+        for k in range(0, each // width, 2):
+            block = (n * (each // width) + k) // 2
+            halves = []
+            for half in range(2):
+                piece = second[(k + half) * width : (k + half + 1) * width, :]
+                piece = piece + jnp.where(slot == 2 * block + half, first, 0.0)
+                if has_prev:
+                    piece = piece + prev_ref[half, block]
+                if keep_total:
+                    total_ref[half, block] = piece
+                halves.append(piece)
+            even = slot % 2 == 0
+            keep_ref[order[block]] = jnp.where(even, halves[0], halves[1])
+            send_ref[order[block]] = jnp.where(even, halves[1], halves[0]).astype(jnp.bfloat16)
 
 
 def step(flat, linear_t, projected, number, cols, low, slot, prev, keep_total, order):
@@ -216,7 +233,7 @@
     args = [slot, low, cols, projected, linear_t, flat]
     if prev is not None:
         args.append(prev)
-    shapes = [jax.ShapeDtypeStruct(full, jnp.bfloat16)]
+    shapes = [jax.ShapeDtypeStruct(full[1:], jnp.float32), jax.ShapeDtypeStruct(full[1:], jnp.bfloat16)]
     if keep_total:
         shapes.append(jax.ShapeDtypeStruct(full, jnp.float32))
     return pl.pallas_call(
@@ -235,21 +252,22 @@
     steps, batch = states.shape[:2]
     slot = jnp.reshape(lax.axis_index(IN), (1,)).astype(jnp.int32)
     own = adjoint_end.T
-    lam = start_rows(own)
+    lam, other = start_rows(own)
+    low = in_order(lam.astype(jnp.bfloat16), other)
     flat, projected, cols = load(
         tensor.reshape(rows * width, modes), states.reshape(steps * batch, modes), slot, width
     )
     order = range(16) if R1 == "A" else [b % 8 * 2 + b // 8 for b in range(16)]
     total = None
     for number in range(steps - 1, -1, -1):
-        low = lax.all_gather(lam.astype(jnp.bfloat16), "core").reshape(rows, batch)
-        send, *rest = step(
+        keep, send, *rest = step(
             flat, linear.T, projected, number, cols, low, slot, total, number > 0, order if number else range(16)
         )
-        half = core_half(send)
+        half = core_half(keep, send)
         if number:
             total = rest[0]
             lam = lam + step_size * to_out_blocks(half)
+            low = lax.all_gather(lam.astype(jnp.bfloat16), "core").reshape(rows, batch)
     return (own + step_size * to_in_blocks(half)).T
 
 

time: 93.1 us -> 99.1 us (1.064)
  starting transfers between devices: 4.4 us -> 16.2 us
  blocking collectives: 77.6 us -> 71 us
    ppermute x1 -> x2, starting transfers between devices: 4.4 us -> 16.2 us  [the longest x1 8.18 us: start_rows(): other = lax.ppermute(own.astype(jnp.bfloat16), AXES, cross)]
    all_to_all x4, blocking collectives: 69.6 us -> 64.6 us  [exchange(): return lax.all_to_all(pieces, axes, 0, 0, tiled=True)]
    all_gather x2 -> x1, blocking collectives: 3.64 us -> 1.82 us  [per_device(): low = lax.all_gather(lam.astype(jnp.bfloat16), 'core').reshape(rows, batch)]
  transfers between devices with their start and end apart: 1 -> 2, of which waited for: 0 -> 0; matrix products, arithmetic and copies ran while one was open for 0% -> 1% of each run, Pallas kernels for 5% -> 4%
where the time goes in v3:
time: 99.1 us; the launch traced here: 98.6 us
  blocking collectives  71 us (72%)
  starting transfers between devices  16.2 us (16%)
  Pallas kernels  6.58 us (7%)
  local copies, waits for them, and re-layouts  3.23 us (3%)
  other arithmetic  1.5 us (2%)
    all_to_all x4, blocking collectives, exchange(): return lax.all_to_all(pieces, axes, 0, 0, tiled=True)  64.6 us
    ppermute x1, starting transfers between devices, start_rows(): other = lax.ppermute(own.astype(jnp.bfloat16), AXES, cross)  8.18 us
    ppermute x1, starting transfers between devices, start_rows(): return (lax.ppermute(own, AXES, same), other)  7.99 us
    all_gather x2, blocking collectives, core_half(): both = lax.all_gather(send, 'core')  4.58 us
    pallas_call x1, Pallas kernels, load(): pl.pallas_call(load_kernel, out_shape=(jax.ShapeDtypeStruct(flat.shape, f...  4.28 us
    unnamed x8, local copies, waits for them, and re-layouts  3.23 us
    pallas_call x2, Pallas kernels, step(): pl.pallas_call(functools.partial(step_kernel, prev is not None, keep_tota...  2.24 us
  transfers between devices with their start and end apart: 2, of which 0 were waited for; matrix products, arithmetic and copies ran while one was open for 1% of the time, Pallas kernels for 4%

profile of v3, /device:TPU:2, one launch (start us, length us, event | category | flops | bytes accessed | tf_op | source)
XLA Modules:
  0.0 98.6 jit_solution(17544178548782686990)
XLA Ops:
  0.0 0.0 copy-start.2
  0.0 8.0 %collective-permute-start = (f32[32,128]{1,0:T(8,128)}, f32[32,128]{1,0:T(8,128)S(1)}, u32[]{:S(2)}, u32[]{:S(2)}) collective-permute-start(f32[32,128]{1,0:T(8,128)} %bitcast.30), channel_id=1, source_target_pairs={{0,4},{1,5},{32,2},{33,3},{64,0},{65,1},{96,14},{97,15},{128,6},{1... | collective-permute-start | bytes 49160 | tf_op jit(solution)/shard_map/ppermute | solution.py:77
  8.0 0.7 bitcast_convert_fusion
  8.7 8.2 %collective-permute-start.1 = (bf16[32,128]{1,0:T(8,128)(2,1)S(1)}, bf16[32,128]{1,0:T(8,128)(2,1)S(1)}, u32[]{:S(2)}, u32[]{:S(2)}) collective-permute-start(bf16[32,128]{1,0:T(8,128)(2,1)S(1)} %bitcast_convert_fusion), channel_id=1, source_target_pairs={{0,5},{1,4},{32,3},{33,2},{64,1},{65,0},{96,15},{97,14},{128,7},{1... | collective-permute-start | bytes 24584 | tf_op jit(solution)/shard_map/ppermute | solution.py:76
  16.9 0.0 copy-start
  16.9 2.2 %copy-done = bf16[64,32,1024]{2,1,0:T(8,128)(2,1)S(1)} copy-done((bf16[64,32,1024]{2,1,0:T(8,128)(2,1)S(1)}, bf16[64,32,1024]{2,1,0:T(8,128)(2,1)}, u32[]{:S(2)}) %copy-start) | copy-done | bytes 4194328
  19.1 0.0 copy-start.1
  19.1 1.0 %copy-done.1 = bf16[2,128,1024]{2,1,0:T(8,128)(2,1)S(1)} copy-done((bf16[2,128,1024]{2,1,0:T(8,128)(2,1)S(1)}, bf16[2,128,1024]{2,1,0:T(8,128)(2,1)}, u32[]{:S(2)}) %copy-start.1) | copy-done | bytes 524312
  20.2 4.3 %load.1 = (bf16[2048,1024]{1,0:T(8,128)(2,1)S(1)}, f32[2048,256]{1,0:T(8,128)S(1)}, f32[32,256]{1,0:T(8,128)S(1)}) custom-call(s32[1]{0:T(128)} %bitcast.slot_ref.refs_0_, bf16[2048,1024]{1,0:T(8,128)(2,1)S(1)} %bitcast.20, bf16[256,1024]{1,0:T(8,128)(2,1)S(1)} %bitcast.22), custom_call_target="tpu_custom_call" | custom-call | tf_op jit(solution)/shard_map/load/pallas_call | solution.py:166
  24.5 0.0 collective-permute-done.1
  24.5 0.0 collective-permute-done
  24.5 0.0 copy-done.2
  24.5 1.1 %step.2 = (f32[16,32,128]{2,1,0:T(8,128)S(1)}, bf16[16,32,128]{2,1,0:T(8,128)(2,1)S(1)}, f32[2,16,32,128]{3,2,1,0:T(8,128)S(1)}) custom-call(s32[1]{0:T(128)} %bitcast.slot_ref.refs_0_, bf16[64,128]{1,0:T(8,128)(2,1)S(1)} %pad_maximum_fusion.refs_1_, f32[32,256]{1,0:T(8,128)S(1)} %get-tuple-element.13.refs_2_, f32[2048,256]{1,0:T(8,128)S(1)} %get-tuple-element.14.refs_3_, ...), custom_call_target="tpu_custom_call" | custom-call | tf_op jit(solution)/shard_map/step/pallas_call | solution.py:239
  25.7 2.6 %all-gather = bf16[32,32,128]{2,1,0:T(8,128)(2,1)S(1)} all-gather(bf16[16,32,128]{2,1,0:T(8,128)(2,1)S(1)} %get-tuple-element.17), channel_id=2, replica_groups=mesh['yhi'=2,'z'=8,'ylo'=4,'x'=4,'core'=2] {'core'}, dimensions={0}, use_global_device_ids=true | all-gather | bytes 393216 | tf_op jit(solution)/shard_map/all_gather | solution.py:86
  28.3 15.4 %all_to_all.20.got_ref = bf16[8,2,32,128]{3,2,1,0:T(8,128)(2,1)S(1)} all-to-all(bf16[8,2,32,128]{3,2,1,0:T(8,128)(2,1)S(1)} %bitcast.29), channel_id=1, replica_groups=mesh['yhi'=2,'z'=8,'ylo'=4,'x'=4,'core'=2] {'z'}, dimensions={0} | all-to-all | bytes 262144 | tf_op jit(solution)/shard_map/all_to_all | solution.py:92
  43.8 20.0 %all_to_all.21 = bf16[32,32,128]{2,1,0:T(8,128)(2,1)S(1)} all-to-all(bf16[32,32,128]{2,1,0:T(8,128)(2,1)S(1)} %bitcast.21), channel_id=1, replica_groups=mesh['yhi'=2,'z'=8,'ylo'=4,'x'=4,'core'=2] {'yhi','ylo','x'}, dimensions={0} | all-to-all | bytes 524288 | tf_op jit(solution)/shard_map/all_to_all | solution.py:92
  63.9 1.8 %all-gather.1.refs_1_ = bf16[64,128]{1,0:T(8,128)(2,1)S(1)} all-gather(bf16[32,128]{1,0:T(8,128)(2,1)S(1)} %add_convert_fusion), channel_id=3, replica_groups=mesh['yhi'=2,'z'=8,'ylo'=4,'x'=4,'core'=2] {'core'}, dimensions={0}, use_global_device_ids=true | all-gather | bytes 24576 | tf_op jit(solution)/shard_map/all_gather | solution.py:270
  65.7 0.0 copy-start.3
  65.7 1.1 %step.3 = (f32[16,32,128]{2,1,0:T(8,128)S(1)}, bf16[16,32,128]{2,1,0:T(8,128)(2,1)S(1)}) custom-call(s32[1]{0:T(128)} %bitcast.slot_ref.refs_0_, bf16[64,128]{1,0:T(8,128)(2,1)S(1)} %all-gather.1.refs_1_, f32[32,256]{1,0:T(8,128)S(1)} %get-tuple-element.13.refs_2_, f32[2048,256]{1,0:T(8,128)S(1)} %get-tuple-element.14.refs_3_, bf16[32,64]{1,0:T(8,128)(2,1)S(1)} %bitcast.26, ...), custom_call_target="tpu_custom_call" | custom-call | tf_op jit(solution)/shard_map/step/pallas_call | solution.py:239
  66.8 2.0 %all-gather.2 = bf16[32,32,128]{2,1,0:T(8,128)(2,1)S(1)} all-gather(bf16[16,32,128]{2,1,0:T(8,128)(2,1)S(1)} %get-tuple-element.20), channel_id=4, replica_groups=mesh['yhi'=2,'z'=8,'ylo'=4,'x'=4,'core'=2] {'core'}, dimensions={0}, use_global_device_ids=true | all-gather | bytes 393216 | tf_op jit(solution)/shard_map/all_gather | solution.py:86
  68.8 12.5 %all_to_all.22 = bf16[16,32,128]{2,1,0:T(8,128)(2,1)S(1)} all-to-all(bf16[16,32,128]{2,1,0:T(8,128)(2,1)S(1)} %fusion), channel_id=1, replica_groups=mesh['yhi'=2,'z'=8,'ylo'=4,'x'=4,'core'=2] {'ylo','x'}, dimensions={0} | all-to-all | bytes 262144 | tf_op jit(solution)/shard_map/all_to_all | solution.py:92
  81.4 16.6 %all_to_all.23 = bf16[16,32,128]{2,1,0:T(8,128)(2,1)S(1)} all-to-all(bf16[16,32,128]{2,1,0:T(8,128)(2,1)S(1)} %bitcast.24), channel_id=1, replica_groups=mesh['yhi'=2,'z'=8,'ylo'=4,'x'=4,'core'=2] {'yhi','z'}, dimensions={0} | all-to-all | bytes 262144 | tf_op jit(solution)/shard_map/all_to_all | solution.py:92
  98.0 0.0 copy-done.3
  98.0 0.6 bitcast_add_fusion
  (9 shorter events, 0.2 us)
Async XLA Ops:
  0.0 24.5 %copy-start.2 = (bf16[64,32]{0,1:T(8,128)(2,1)S(1)}, bf16[64,32]{0,1:T(8,128)(2,1)}, u32[]{:S(2)}) copy-start(bf16[64,32]{0,1:T(8,128)(2,1)} %param.5) | copy-start | bytes 12292
  0.0 24.5 %collective-permute-start = (f32[32,128]{1,0:T(8,128)}, f32[32,128]{1,0:T(8,128)S(1)}, u32[]{:S(2)}, u32[]{:S(2)}) collective-permute-start(f32[32,128]{1,0:T(8,128)} %bitcast.30), channel_id=1, source_target_pairs={{0,4},{1,5},{32,2},{33,3},{64,0},{65,1},{96,14},{97,15},{128,6},{1... | collective-permute-start | bytes 49160 | tf_op jit(solution)/shard_map/ppermute | solution.py:77
  8.7 15.7 %collective-permute-start.1 = (bf16[32,128]{1,0:T(8,128)(2,1)S(1)}, bf16[32,128]{1,0:T(8,128)(2,1)S(1)}, u32[]{:S(2)}, u32[]{:S(2)}) collective-permute-start(bf16[32,128]{1,0:T(8,128)(2,1)S(1)} %bitcast_convert_fusion), channel_id=1, source_target_pairs={{0,5},{1,4},{32,3},{33,2},{64,1},{65,0},{96,15},{97,14},{128,7},{1... | collective-permute-start | bytes 24584 | tf_op jit(solution)/shard_map/ppermute | solution.py:76
  16.9 2.2 %copy-start = (bf16[64,32,1024]{2,1,0:T(8,128)(2,1)S(1)}, bf16[64,32,1024]{2,1,0:T(8,128)(2,1)}, u32[]{:S(2)}) copy-start(bf16[64,32,1024]{2,1,0:T(8,128)(2,1)} %param.4) | copy-start | bytes 12582916
  19.1 1.0 %copy-start.1 = (bf16[2,128,1024]{2,1,0:T(8,128)(2,1)S(1)}, bf16[2,128,1024]{2,1,0:T(8,128)(2,1)}, u32[]{:S(2)}) copy-start(bf16[2,128,1024]{2,1,0:T(8,128)(2,1)} %param.7) | copy-start | bytes 1572868
  65.7 32.3 %copy-start.3 = (f32[128,32]{0,1:T(8,128)S(1)}, f32[128,32]{0,1:T(8,128)}, u32[]{:S(2)}) copy-start(f32[128,32]{0,1:T(8,128)} %param.6) | copy-start | bytes 49156

commit v4 on v3

--- a/solution.py
+++ b/solution.py
@@ -10,14 +10,13 @@
 
 step_size = 0.5
 VMEM = pl.BlockSpec(memory_space=pltpu.VMEM)
-HBM = pl.BlockSpec(memory_space=pltpu.HBM)
 SMEM = pl.BlockSpec(memory_space=pltpu.SMEM)
 LIMIT = 16 * 1024 * 1024
 AXES = ("yhi", "z", "ylo", "x", "core")
 SIZES = (2, 8, 4, 4, 2)
 OUT = ("yhi", "z")
 IN = ("ylo", "x", "core")
-CHIP = ("ylo", "x")
+CHIP = ("x", "ylo")
 PLANE = ("yhi", "ylo", "x")
 R1 = "B"
 R0 = "A"
@@ -49,37 +48,45 @@
 
 def assign(cost):
     n = len(cost)
-    for limit in range(int(cost.max()) + 1):
-        owner = [-1] * n
-
-        def place(i, seen):
-            for j in sorted(range(n), key=lambda k: cost[i][k]):
-                if cost[i][j] <= limit and j not in seen:
-                    seen.add(j)
-                    if owner[j] < 0 or place(owner[j], seen):
-                        owner[j] = i
-                        return True
-            return False
-
-        if all(place(i, set()) for i in range(n)):
-            match = [0] * n
-            for j, i in enumerate(owner):
-                match[i] = j
-            return match
-    raise ValueError("no matching")
+    weight = cost.astype(np.int64) ** 4
+    row_of = [-1] * n
+    high, low = [0] * (n + 1), [0] * (n + 1)
+    match = [n] * (n + 1)
+    for i in range(n):
+        match[n] = i
+        col = n
+        least = [1 << 60] * (n + 1)
+        back = [n] * (n + 1)
+        used = [False] * (n + 1)
+        while match[col] != n:
+            used[col] = True
+            row, delta, nxt = match[col], 1 << 60, n
+            for j in range(n):
+                if not used[j]:
+                    reduced = int(weight[row][j]) - high[row] - low[j]
+                    if reduced < least[j]:
+                        least[j], back[j] = reduced, col
+                    if least[j] < delta:
+                        delta, nxt = least[j], j
+            for j in range(n + 1):
+                if used[j]:
+                    high[match[j]] += delta
+                    low[j] -= delta
+                else:
+                    least[j] -= delta
+            col = nxt
+        while col != n:
+            prev = back[col]
+            match[col] = match[prev]
+            col = prev
+    for j in range(n):
+        row_of[match[j]] = j
+    return row_of
 
 
 def start_rows(own):
-    pairs = spread_pairs()
-    same = [(2 * a + c, 2 * b + c) for a, b in pairs for c in range(2)]
-    cross = [(2 * a + c, 2 * b + 1 - c) for a, b in pairs for c in range(2)]
-    other = lax.ppermute(own.astype(jnp.bfloat16), AXES, cross)
-    return lax.ppermute(own, AXES, same), other
-
-
-def in_order(mine, other):
-    first = lax.axis_index("core") == 0
-    return jnp.concatenate([jnp.where(first, mine, other), jnp.where(first, other, mine)], 0)
+    perm = [(2 * a + c, 2 * b + c) for a, b in spread_pairs() for c in range(2)]
+    return lax.ppermute(own, AXES, perm)
 
 
 def core_half(keep, send):
@@ -134,30 +141,16 @@
     return total_of(exchange(fold(exchange(both, PLANE)[:, None], 8), "z"))
 
 
-CHUNKS = 8
-
-def load_kernel(slot_ref, tensor_ref, source_ref, kept_ref, projected_ref, cols_ref, states_ref, sems):
-    height = kept_ref.shape[0] // CHUNKS
-    first = pltpu.make_async_copy(source_ref, states_ref, sems.at[CHUNKS])
-    first.start()
-    loads = []
-    for c in range(CHUNKS):
-        rows = pl.ds(c * height, height)
-        loads.append(pltpu.make_async_copy(tensor_ref.at[rows], kept_ref.at[rows], sems.at[c]))
-        loads[-1].start()
-    first.wait()
+def load_kernel(slot_ref, tensor_ref, states_ref, projected_ref, cols_ref):
     states = states_ref[...]
     shape = (cols_ref.shape[0], states.shape[1])
     wanted = lax.broadcasted_iota(jnp.int32, shape, 0) + slot_ref[0] * shape[0]
     pick = (lax.broadcasted_iota(jnp.int32, shape, 1) == wanted).astype(jnp.bfloat16)
     along = (((1,), (1,)), ((), ()))
     cols_ref[...] = lax.dot_general(pick, states, along, preferred_element_type=jnp.float32)
-    for c in range(CHUNKS):
-        loads[c].wait()
-        rows = slice(c * height, (c + 1) * height)
-        projected_ref[rows, :] = lax.dot_general(
-            kept_ref[rows, :], states, along, preferred_element_type=jnp.float32
-        )
+    projected_ref[...] = lax.dot_general(
+        tensor_ref[...], states, along, preferred_element_type=jnp.float32
+    )
 
 
 def load(flat, states, slot, width):
@@ -166,13 +159,11 @@
     return pl.pallas_call(
         load_kernel,
         out_shape=(
-            jax.ShapeDtypeStruct(flat.shape, flat.dtype),
             jax.ShapeDtypeStruct((height, count), jnp.float32),
             jax.ShapeDtypeStruct((width, count), jnp.float32),
         ),
-        in_specs=[SMEM, HBM, HBM],
-        out_specs=(VMEM, VMEM, VMEM),
-        scratch_shapes=[pltpu.VMEM(states.shape, states.dtype), pltpu.SemaphoreType.DMA((CHUNKS + 1,))],
+        in_specs=[SMEM, VMEM, VMEM],
+        out_specs=(VMEM, VMEM),
         compiler_params=pltpu.CompilerParams(vmem_limit_bytes=LIMIT),
         name="load",
     )(slot, flat, states)
@@ -252,22 +243,21 @@
     steps, batch = states.shape[:2]
     slot = jnp.reshape(lax.axis_index(IN), (1,)).astype(jnp.int32)
     own = adjoint_end.T
-    lam, other = start_rows(own)
-    low = in_order(lam.astype(jnp.bfloat16), other)
-    flat, projected, cols = load(
-        tensor.reshape(rows * width, modes), states.reshape(steps * batch, modes), slot, width
-    )
+    lam = start_rows(own)
+    flat = tensor.reshape(rows * width, modes)
+    projected, cols = load(flat, states.reshape(steps * batch, modes), slot, width)
     order = range(16) if R1 == "A" else [b % 8 * 2 + b // 8 for b in range(16)]
+    last = [b % 4 * 4 + b // 4 for b in range(16)]
     total = None
     for number in range(steps - 1, -1, -1):
+        low = lax.all_gather(lam.astype(jnp.bfloat16), "core").reshape(rows, batch)
         keep, send, *rest = step(
-            flat, linear.T, projected, number, cols, low, slot, total, number > 0, order if number else range(16)
+            flat, linear.T, projected, number, cols, low, slot, total, number > 0, order if number else last
         )
         half = core_half(keep, send)
         if number:
             total = rest[0]
             lam = lam + step_size * to_out_blocks(half)
-            low = lax.all_gather(lam.astype(jnp.bfloat16), "core").reshape(rows, batch)
     return (own + step_size * to_in_blocks(half)).T
 
 

time: 99.1 us -> 92.2 us (0.930)
  the two profiles are of different devices: /device:TPU:2 before, /device:TPU:8 now
where the time goes in v4:
time: 92.2 us; the launch traced here: 91.8 us
  blocking collectives  72.9 us (79%)
  starting transfers between devices  11 us (12%)
  Pallas kernels  3.74 us (4%)
  local copies, waits for them, and re-layouts  3.24 us (4%)
    all_to_all x4, blocking collectives, exchange(): return lax.all_to_all(pieces, axes, 0, 0, tiled=True)  65.2 us
    ppermute x1, starting transfers between devices, start_rows(): return lax.ppermute(own, AXES, perm)  11 us
    all_gather x2, blocking collectives, core_half(): both = lax.all_gather(send, 'core')  4.12 us
    all_gather x2, blocking collectives, per_device(): low = lax.all_gather(lam.astype(jnp.bfloat16), 'core').reshape(rows, batch)  3.64 us
    unnamed x10, local copies, waits for them, and re-layouts  3.24 us
    pallas_call x2, Pallas kernels, step(): pl.pallas_call(functools.partial(step_kernel, prev is not None, keep_tota...  2.21 us
  transfers between devices with their start and end apart: 1, of which 0 were waited for; matrix products, arithmetic and copies ran while one was open for 0% of the time, Pallas kernels for 2%

profile of v4, /device:TPU:8, one launch (start us, length us, event | category | flops | bytes accessed | tf_op | source)
XLA Modules:
  0.0 91.8 jit_solution(18346066338517975481)
XLA Ops:
  0.0 0.0 copy-start.3
  0.0 11.0 %collective-permute-start = (f32[32,128]{1,0:T(8,128)}, f32[32,128]{1,0:T(8,128)S(1)}, u32[]{:S(2)}, u32[]{:S(2)}) collective-permute-start(f32[32,128]{1,0:T(8,128)} %bitcast.31), channel_id=1, source_target_pairs={{0,12},{1,13},{32,10},{33,11},{64,8},{65,9},{96,2},{97,3},{128,0},... | collective-permute-start | bytes 49160 | tf_op jit(solution)/shard_map/ppermute | solution.py:89
  11.1 0.0 copy-start
  11.1 2.2 %copy-done = bf16[64,32,1024]{2,1,0:T(8,128)(2,1)S(1)} copy-done((bf16[64,32,1024]{2,1,0:T(8,128)(2,1)S(1)}, bf16[64,32,1024]{2,1,0:T(8,128)(2,1)}, u32[]{:S(2)}) %copy-start) | copy-done | bytes 4194328
  13.2 0.0 copy-start.2
  13.3 1.0 %copy-done.2 = bf16[2,128,1024]{2,1,0:T(8,128)(2,1)S(1)} copy-done((bf16[2,128,1024]{2,1,0:T(8,128)(2,1)S(1)}, bf16[2,128,1024]{2,1,0:T(8,128)(2,1)}, u32[]{:S(2)}) %copy-start.2) | copy-done | bytes 524312
  14.3 1.5 %load.1 = (f32[2048,256]{1,0:T(8,128)S(1)}, f32[32,256]{1,0:T(8,128)S(1)}) custom-call(s32[1]{0:T(128)} %bitcast.slot_ref.refs_0_, bf16[2048,1024]{1,0:T(8,128)(2,1)S(1)} %bitcast.19, bf16[256,1024]{1,0:T(8,128)(2,1)S(1)} %bitcast.23), custom_call_target="tpu_custom_call" | custom-call | tf_op jit(solution)/shard_map/load/pallas_call | solution.py:159
  15.8 0.0 collective-permute-done
  15.8 1.8 %all-gather.refs_1_ = bf16[64,128]{1,0:T(8,128)(2,1)S(1)} all-gather(bf16[32,128]{1,0:T(8,128)(2,1)S(1)} %convert_element_type.30), channel_id=2, replica_groups=mesh['yhi'=2,'z'=8,'ylo'=4,'x'=4,'core'=2] {'core'}, dimensions={0}, use_global_device_ids=true | all-gather | bytes 24576 | tf_op jit(solution)/shard_map/all_gather | solution.py:253
  17.6 0.0 copy-done.3
  17.6 0.0 copy-start.1
  17.6 1.1 %step.2 = (f32[16,32,128]{2,1,0:T(8,128)S(1)}, bf16[16,32,128]{2,1,0:T(8,128)(2,1)S(1)}, f32[2,16,32,128]{3,2,1,0:T(8,128)S(1)}) custom-call(s32[1]{0:T(128)} %bitcast.slot_ref.refs_0_, bf16[64,128]{1,0:T(8,128)(2,1)S(1)} %all-gather.refs_1_, f32[32,256]{1,0:T(8,128)S(1)} %get-tuple-element.12.refs_2_, f32[2048,256]{1,0:T(8,128)S(1)} %get-tuple-element.13.refs_3_, ...), custom_call_target="tpu_custom_call" | custom-call | tf_op jit(solution)/shard_map/step/pallas_call | solution.py:230
  18.8 2.1 %all-gather.1 = bf16[32,32,128]{2,1,0:T(8,128)(2,1)S(1)} all-gather(bf16[16,32,128]{2,1,0:T(8,128)(2,1)S(1)} %get-tuple-element.15), channel_id=3, replica_groups=mesh['yhi'=2,'z'=8,'ylo'=4,'x'=4,'core'=2] {'core'}, dimensions={0}, use_global_device_ids=true | all-gather | bytes 393216 | tf_op jit(solution)/shard_map/all_gather | solution.py:93
  20.9 14.5 %all_to_all.20.got_ref = bf16[8,2,32,128]{3,2,1,0:T(8,128)(2,1)S(1)} all-to-all(bf16[8,2,32,128]{3,2,1,0:T(8,128)(2,1)S(1)} %bitcast.30), channel_id=1, replica_groups=mesh['yhi'=2,'z'=8,'ylo'=4,'x'=4,'core'=2] {'z'}, dimensions={0} | all-to-all | bytes 262144 | tf_op jit(solution)/shard_map/all_to_all | solution.py:99
  35.5 22.5 %all_to_all.21 = bf16[32,32,128]{2,1,0:T(8,128)(2,1)S(1)} all-to-all(bf16[32,32,128]{2,1,0:T(8,128)(2,1)S(1)} %bitcast.22), channel_id=1, replica_groups=mesh['yhi'=2,'z'=8,'ylo'=4,'x'=4,'core'=2] {'yhi','ylo','x'}, dimensions={0} | all-to-all | bytes 524288 | tf_op jit(solution)/shard_map/all_to_all | solution.py:99
  58.0 1.8 %all-gather.2.refs_1_ = bf16[64,128]{1,0:T(8,128)(2,1)S(1)} all-gather(bf16[32,128]{1,0:T(8,128)(2,1)S(1)} %add_convert_fusion), channel_id=4, replica_groups=mesh['yhi'=2,'z'=8,'ylo'=4,'x'=4,'core'=2] {'core'}, dimensions={0}, use_global_device_ids=true | all-gather | bytes 24576 | tf_op jit(solution)/shard_map/all_gather | solution.py:253
  59.8 0.0 copy-done.1
  59.8 0.0 copy-start.4
  59.8 1.1 %step.3 = (f32[16,32,128]{2,1,0:T(8,128)S(1)}, bf16[16,32,128]{2,1,0:T(8,128)(2,1)S(1)}) custom-call(s32[1]{0:T(128)} %bitcast.slot_ref.refs_0_, bf16[64,128]{1,0:T(8,128)(2,1)S(1)} %all-gather.2.refs_1_, f32[32,256]{1,0:T(8,128)S(1)} %get-tuple-element.12.refs_2_, f32[2048,256]{1,0:T(8,128)S(1)} %get-tuple-element.13.refs_3_, bf16[32,64]{1,0:T(8,128)(2,1)S(1)} %bitcast.27, ...), custom_call_target="tpu_custom_call" | custom-call | tf_op jit(solution)/shard_map/step/pallas_call | solution.py:230
  60.9 2.0 %all-gather.3 = bf16[32,32,128]{2,1,0:T(8,128)(2,1)S(1)} all-gather(bf16[16,32,128]{2,1,0:T(8,128)(2,1)S(1)} %get-tuple-element.18), channel_id=5, replica_groups=mesh['yhi'=2,'z'=8,'ylo'=4,'x'=4,'core'=2] {'core'}, dimensions={0}, use_global_device_ids=true | all-gather | bytes 393216 | tf_op jit(solution)/shard_map/all_gather | solution.py:93
  62.9 11.2 %all_to_all.22 = bf16[16,32,128]{2,1,0:T(8,128)(2,1)S(1)} all-to-all(bf16[16,32,128]{2,1,0:T(8,128)(2,1)S(1)} %fusion), channel_id=1, replica_groups=mesh['yhi'=2,'z'=8,'ylo'=4,'x'=4,'core'=2] {'x','ylo'}, dimensions={0} | all-to-all | bytes 262144 | tf_op jit(solution)/shard_map/all_to_all | solution.py:99
  74.2 17.0 %all_to_all.23 = bf16[16,32,128]{2,1,0:T(8,128)(2,1)S(1)} all-to-all(bf16[16,32,128]{2,1,0:T(8,128)(2,1)S(1)} %bitcast.25), channel_id=1, replica_groups=mesh['yhi'=2,'z'=8,'ylo'=4,'x'=4,'core'=2] {'yhi','z'}, dimensions={0} | all-to-all | bytes 262144 | tf_op jit(solution)/shard_map/all_to_all | solution.py:99
  91.2 0.0 copy-done.4
  91.2 0.6 bitcast_add_fusion
  (8 shorter events, 0.2 us)
Async XLA Ops:
  0.0 17.6 %copy-start.3 = (bf16[64,32]{0,1:T(8,128)(2,1)S(1)}, bf16[64,32]{0,1:T(8,128)(2,1)}, u32[]{:S(2)}) copy-start(bf16[64,32]{0,1:T(8,128)(2,1)} %param.5) | copy-start | bytes 12292
  0.0 15.8 %collective-permute-start = (f32[32,128]{1,0:T(8,128)}, f32[32,128]{1,0:T(8,128)S(1)}, u32[]{:S(2)}, u32[]{:S(2)}) collective-permute-start(f32[32,128]{1,0:T(8,128)} %bitcast.31), channel_id=1, source_target_pairs={{0,12},{1,13},{32,10},{33,11},{64,8},{65,9},{96,2},{97,3},{128,0},... | collective-permute-start | bytes 49160 | tf_op jit(solution)/shard_map/ppermute | solution.py:89
  11.1 2.2 %copy-start = (bf16[64,32,1024]{2,1,0:T(8,128)(2,1)S(1)}, bf16[64,32,1024]{2,1,0:T(8,128)(2,1)}, u32[]{:S(2)}) copy-start(bf16[64,32,1024]{2,1,0:T(8,128)(2,1)} %param.4) | copy-start | bytes 12582916
  13.2 1.0 %copy-start.2 = (bf16[2,128,1024]{2,1,0:T(8,128)(2,1)S(1)}, bf16[2,128,1024]{2,1,0:T(8,128)(2,1)}, u32[]{:S(2)}) copy-start(bf16[2,128,1024]{2,1,0:T(8,128)(2,1)} %param.7) | copy-start | bytes 1572868
  17.6 42.2 %copy-start.1 = (bf16[64,32,1024]{2,1,0:T(8,128)(2,1)S(1)}, bf16[64,32,1024]{2,1,0:T(8,128)(2,1)}, u32[]{:S(2)}) copy-start(bf16[64,32,1024]{2,1,0:T(8,128)(2,1)} %param.4) | copy-start | bytes 12582916
  59.8 31.4 %copy-start.4 = (f32[128,32]{0,1:T(8,128)S(1)}, f32[128,32]{0,1:T(8,128)}, u32[]{:S(2)}) copy-start(f32[128,32]{0,1:T(8,128)} %param.6) | copy-start | bytes 49156

commit v5 on v4

--- a/solution.py
+++ b/solution.py
@@ -18,7 +18,7 @@
 IN = ("ylo", "x", "core")
 CHIP = ("x", "ylo")
 PLANE = ("yhi", "ylo", "x")
-R1 = "B"
+R1 = "A"
 R0 = "A"
 
 

time: 92.2 us -> 90.9 us (0.986)
  blocking collectives: 72.9 us -> 71.6 us
    all_to_all x4, blocking collectives: 65.2 us -> 63.8 us  [exchange(): return lax.all_to_all(pieces, axes, 0, 0, tiled=True)]
where the time goes in v5:
time: 90.9 us; the launch traced here: 90.5 us
  blocking collectives  71.6 us (79%)
  starting transfers between devices  11 us (12%)
  Pallas kernels  3.74 us (4%)
  local copies, waits for them, and re-layouts  3.24 us (4%)
    all_to_all x4, blocking collectives, exchange(): return lax.all_to_all(pieces, axes, 0, 0, tiled=True)  63.8 us
    ppermute x1, starting transfers between devices, start_rows(): return lax.ppermute(own, AXES, perm)  11 us
    all_gather x2, blocking collectives, core_half(): both = lax.all_gather(send, 'core')  3.99 us
    all_gather x2, blocking collectives, per_device(): low = lax.all_gather(lam.astype(jnp.bfloat16), 'core').reshape(rows, batch)  3.77 us
    unnamed x10, local copies, waits for them, and re-layouts  3.24 us
    pallas_call x2, Pallas kernels, step(): pl.pallas_call(functools.partial(step_kernel, prev is not None, keep_tota...  2.21 us
  transfers between devices with their start and end apart: 1, of which 0 were waited for; matrix products, arithmetic and copies ran while one was open for 0% of the time, Pallas kernels for 2%

profile of v5, /device:TPU:8, one launch (start us, length us, event | category | flops | bytes accessed | tf_op | source)
XLA Modules:
  0.0 90.5 jit_solution(11667151155334685916)
XLA Ops:
  0.0 0.0 copy-start.3
  0.0 11.0 %collective-permute-start = (f32[32,128]{1,0:T(8,128)}, f32[32,128]{1,0:T(8,128)S(1)}, u32[]{:S(2)}, u32[]{:S(2)}) collective-permute-start(f32[32,128]{1,0:T(8,128)} %bitcast.31), channel_id=1, source_target_pairs={{0,12},{1,13},{32,10},{33,11},{64,8},{65,9},{96,2},{97,3},{128,0},... | collective-permute-start | bytes 49160 | tf_op jit(solution)/shard_map/ppermute | solution.py:89
  11.1 0.0 copy-start
  11.1 2.2 %copy-done = bf16[64,32,1024]{2,1,0:T(8,128)(2,1)S(1)} copy-done((bf16[64,32,1024]{2,1,0:T(8,128)(2,1)S(1)}, bf16[64,32,1024]{2,1,0:T(8,128)(2,1)}, u32[]{:S(2)}) %copy-start) | copy-done | bytes 4194328
  13.2 0.0 copy-start.2
  13.3 1.0 %copy-done.2 = bf16[2,128,1024]{2,1,0:T(8,128)(2,1)S(1)} copy-done((bf16[2,128,1024]{2,1,0:T(8,128)(2,1)S(1)}, bf16[2,128,1024]{2,1,0:T(8,128)(2,1)}, u32[]{:S(2)}) %copy-start.2) | copy-done | bytes 524312
  14.3 1.5 %load.1 = (f32[2048,256]{1,0:T(8,128)S(1)}, f32[32,256]{1,0:T(8,128)S(1)}) custom-call(s32[1]{0:T(128)} %bitcast.slot_ref.refs_0_, bf16[2048,1024]{1,0:T(8,128)(2,1)S(1)} %bitcast.19, bf16[256,1024]{1,0:T(8,128)(2,1)S(1)} %bitcast.22), custom_call_target="tpu_custom_call" | custom-call | tf_op jit(solution)/shard_map/load/pallas_call | solution.py:159
  15.8 0.0 copy-start.1
  15.8 0.0 collective-permute-done
  15.8 2.0 %all-gather.refs_1_ = bf16[64,128]{1,0:T(8,128)(2,1)S(1)} all-gather(bf16[32,128]{1,0:T(8,128)(2,1)S(1)} %convert_element_type.30), channel_id=2, replica_groups=mesh['yhi'=2,'z'=8,'ylo'=4,'x'=4,'core'=2] {'core'}, dimensions={0}, use_global_device_ids=true | all-gather | bytes 24576 | tf_op jit(solution)/shard_map/all_gather | solution.py:253
  17.8 0.0 copy-done.3
  17.8 1.1 %step.2 = (f32[16,32,128]{2,1,0:T(8,128)S(1)}, bf16[16,32,128]{2,1,0:T(8,128)(2,1)S(1)}, f32[2,16,32,128]{3,2,1,0:T(8,128)S(1)}) custom-call(s32[1]{0:T(128)} %bitcast.slot_ref.refs_0_, bf16[64,128]{1,0:T(8,128)(2,1)S(1)} %all-gather.refs_1_, f32[32,256]{1,0:T(8,128)S(1)} %get-tuple-element.12.refs_2_, f32[2048,256]{1,0:T(8,128)S(1)} %get-tuple-element.13.refs_3_, ...), custom_call_target="tpu_custom_call" | custom-call | tf_op jit(solution)/shard_map/step/pallas_call | solution.py:230
  18.9 2.0 %all-gather.1 = bf16[32,32,128]{2,1,0:T(8,128)(2,1)S(1)} all-gather(bf16[16,32,128]{2,1,0:T(8,128)(2,1)S(1)} %get-tuple-element.15), channel_id=3, replica_groups=mesh['yhi'=2,'z'=8,'ylo'=4,'x'=4,'core'=2] {'core'}, dimensions={0}, use_global_device_ids=true | all-gather | bytes 393216 | tf_op jit(solution)/shard_map/all_gather | solution.py:93
  20.9 23.3 %all_to_all.20 = bf16[16,32,128]{2,1,0:T(8,128)(2,1)S(1)} all-to-all(bf16[16,32,128]{2,1,0:T(8,128)(2,1)S(1)} %fusion.1), channel_id=1, replica_groups=mesh['yhi'=2,'z'=8,'ylo'=4,'x'=4,'core'=2] {'yhi','z'}, dimensions={0} | all-to-all | bytes 262144 | tf_op jit(solution)/shard_map/all_to_all | solution.py:99
  44.2 13.1 %all_to_all.21 = bf16[16,32,128]{2,1,0:T(8,128)(2,1)S(1)} all-to-all(bf16[16,32,128]{2,1,0:T(8,128)(2,1)S(1)} %bitcast.24), channel_id=1, replica_groups=mesh['yhi'=2,'z'=8,'ylo'=4,'x'=4,'core'=2] {'x','ylo'}, dimensions={0} | all-to-all | bytes 262144 | tf_op jit(solution)/shard_map/all_to_all | solution.py:99
  57.4 1.8 %all-gather.2.refs_1_ = bf16[64,128]{1,0:T(8,128)(2,1)S(1)} all-gather(bf16[32,128]{1,0:T(8,128)(2,1)S(1)} %add_convert_fusion), channel_id=4, replica_groups=mesh['yhi'=2,'z'=8,'ylo'=4,'x'=4,'core'=2] {'core'}, dimensions={0}, use_global_device_ids=true | all-gather | bytes 24576 | tf_op jit(solution)/shard_map/all_gather | solution.py:253
  59.2 0.0 copy-done.1
  59.2 0.0 copy-start.4
  59.2 1.1 %step.3 = (f32[16,32,128]{2,1,0:T(8,128)S(1)}, bf16[16,32,128]{2,1,0:T(8,128)(2,1)S(1)}) custom-call(s32[1]{0:T(128)} %bitcast.slot_ref.refs_0_, bf16[64,128]{1,0:T(8,128)(2,1)S(1)} %all-gather.2.refs_1_, f32[32,256]{1,0:T(8,128)S(1)} %get-tuple-element.12.refs_2_, f32[2048,256]{1,0:T(8,128)S(1)} %get-tuple-element.13.refs_3_, bf16[32,64]{1,0:T(8,128)(2,1)S(1)} %bitcast.28, ...), custom_call_target="tpu_custom_call" | custom-call | tf_op jit(solution)/shard_map/step/pallas_call | solution.py:230
  60.3 2.0 %all-gather.3 = bf16[32,32,128]{2,1,0:T(8,128)(2,1)S(1)} all-gather(bf16[16,32,128]{2,1,0:T(8,128)(2,1)S(1)} %get-tuple-element.18), channel_id=5, replica_groups=mesh['yhi'=2,'z'=8,'ylo'=4,'x'=4,'core'=2] {'core'}, dimensions={0}, use_global_device_ids=true | all-gather | bytes 393216 | tf_op jit(solution)/shard_map/all_gather | solution.py:93
  62.4 11.2 %all_to_all.22 = bf16[16,32,128]{2,1,0:T(8,128)(2,1)S(1)} all-to-all(bf16[16,32,128]{2,1,0:T(8,128)(2,1)S(1)} %fusion), channel_id=1, replica_groups=mesh['yhi'=2,'z'=8,'ylo'=4,'x'=4,'core'=2] {'x','ylo'}, dimensions={0} | all-to-all | bytes 262144 | tf_op jit(solution)/shard_map/all_to_all | solution.py:99
  73.6 16.2 %all_to_all.23 = bf16[16,32,128]{2,1,0:T(8,128)(2,1)S(1)} all-to-all(bf16[16,32,128]{2,1,0:T(8,128)(2,1)S(1)} %bitcast.26), channel_id=1, replica_groups=mesh['yhi'=2,'z'=8,'ylo'=4,'x'=4,'core'=2] {'yhi','z'}, dimensions={0} | all-to-all | bytes 262144 | tf_op jit(solution)/shard_map/all_to_all | solution.py:99
  89.8 0.0 copy-done.4
  89.8 0.6 bitcast_add_fusion
  (8 shorter events, 0.2 us)
Async XLA Ops:
  0.0 17.8 %copy-start.3 = (bf16[64,32]{0,1:T(8,128)(2,1)S(1)}, bf16[64,32]{0,1:T(8,128)(2,1)}, u32[]{:S(2)}) copy-start(bf16[64,32]{0,1:T(8,128)(2,1)} %param.5) | copy-start | bytes 12292
  0.0 15.8 %collective-permute-start = (f32[32,128]{1,0:T(8,128)}, f32[32,128]{1,0:T(8,128)S(1)}, u32[]{:S(2)}, u32[]{:S(2)}) collective-permute-start(f32[32,128]{1,0:T(8,128)} %bitcast.31), channel_id=1, source_target_pairs={{0,12},{1,13},{32,10},{33,11},{64,8},{65,9},{96,2},{97,3},{128,0},... | collective-permute-start | bytes 49160 | tf_op jit(solution)/shard_map/ppermute | solution.py:89
  11.1 2.2 %copy-start = (bf16[64,32,1024]{2,1,0:T(8,128)(2,1)S(1)}, bf16[64,32,1024]{2,1,0:T(8,128)(2,1)}, u32[]{:S(2)}) copy-start(bf16[64,32,1024]{2,1,0:T(8,128)(2,1)} %param.4) | copy-start | bytes 12582916
  13.2 1.0 %copy-start.2 = (bf16[2,128,1024]{2,1,0:T(8,128)(2,1)S(1)}, bf16[2,128,1024]{2,1,0:T(8,128)(2,1)}, u32[]{:S(2)}) copy-start(bf16[2,128,1024]{2,1,0:T(8,128)(2,1)} %param.7) | copy-start | bytes 1572868
  15.8 43.4 %copy-start.1 = (bf16[64,32,1024]{2,1,0:T(8,128)(2,1)S(1)}, bf16[64,32,1024]{2,1,0:T(8,128)(2,1)}, u32[]{:S(2)}) copy-start(bf16[64,32,1024]{2,1,0:T(8,128)(2,1)} %param.4) | copy-start | bytes 12582916
  59.2 30.6 %copy-start.4 = (f32[128,32]{0,1:T(8,128)S(1)}, f32[128,32]{0,1:T(8,128)}, u32[]{:S(2)}) copy-start(f32[128,32]{0,1:T(8,128)} %param.6) | copy-start | bytes 49156

commit v6 on v5

--- a/solution.py
+++ b/solution.py
@@ -7,6 +7,7 @@
 from jax.experimental import pallas as pl
 from jax.experimental.pallas import tpu as pltpu
 from jax.sharding import Mesh, PartitionSpec as P
+
 
 step_size = 0.5
 VMEM = pl.BlockSpec(memory_space=pltpu.VMEM)
@@ -89,10 +90,22 @@
     return lax.ppermute(own, AXES, perm)
 
 
-def core_half(keep, send):
+def join_kernel(slot_ref, keep_ref, both_ref, half_ref):
+    even = slot_ref[0] % 2 == 0
+    got = jnp.where(even, both_ref[1].astype(jnp.float32), both_ref[0].astype(jnp.float32))
+    half_ref[...] = (keep_ref[...] + got).astype(jnp.bfloat16)
+
+
+def core_half(keep, send, slot):
     both = lax.all_gather(send, "core")
-    got = lax.dynamic_index_in_dim(both, 1 - lax.axis_index("core"), 0, keepdims=False)
-    return (keep + got.astype(jnp.float32)).astype(jnp.bfloat16)
+    return pl.pallas_call(
+        join_kernel,
+        out_shape=jax.ShapeDtypeStruct(keep.shape, jnp.bfloat16),
+        in_specs=[SMEM, VMEM, VMEM],
+        out_specs=VMEM,
+        compiler_params=pltpu.CompilerParams(vmem_limit_bytes=LIMIT),
+        name="join",
+    )(slot, keep, both)
 
 
 def exchange(pieces, axes):
@@ -141,37 +154,77 @@
     return total_of(exchange(fold(exchange(both, PLANE)[:, None], 8), "z"))
 
 
-def load_kernel(slot_ref, tensor_ref, states_ref, projected_ref, cols_ref):
+ALONG = (((1,), (1,)), ((), ()))
+
+
+def split_kernel(slot_ref, tensor_ref, mine_ref, give_ref):
+    height = mine_ref.shape[0]
+    core = slot_ref[0] % 2
+    mine_ref[...] = tensor_ref[pl.ds(pl.multiple_of(core * height, height), height), :]
+    give_ref[...] = tensor_ref[pl.ds(pl.multiple_of((1 - core) * height, height), height), :]
+
+
+def split(flat, slot):
+    part = jax.ShapeDtypeStruct((flat.shape[0] // 2, flat.shape[1]), flat.dtype)
+    return pl.pallas_call(
+        split_kernel,
+        out_shape=(part, part),
+        in_specs=[SMEM, VMEM],
+        out_specs=(VMEM, VMEM),
+        compiler_params=pltpu.CompilerParams(vmem_limit_bytes=LIMIT),
+        name="split",
+    )(slot, flat)
+
+
+def load_kernel(slot_ref, mine_ref, states_ref, projected_ref, cols_ref):
     states = states_ref[...]
-    shape = (cols_ref.shape[0], states.shape[1])
-    wanted = lax.broadcasted_iota(jnp.int32, shape, 0) + slot_ref[0] * shape[0]
-    pick = (lax.broadcasted_iota(jnp.int32, shape, 1) == wanted).astype(jnp.bfloat16)
-    along = (((1,), (1,)), ((), ()))
-    cols_ref[...] = lax.dot_general(pick, states, along, preferred_element_type=jnp.float32)
-    projected_ref[...] = lax.dot_general(
-        tensor_ref[...], states, along, preferred_element_type=jnp.float32
-    )
-
-
-def load(flat, states, slot, width):
-    height, modes = flat.shape
+    width = cols_ref.shape[0] // 2
+    slot = slot_ref[0]
+    shape = (width, states.shape[1])
+    for part, place in enumerate((slot, slot + 1 - 2 * (slot % 2))):
+        wanted = lax.broadcasted_iota(jnp.int32, shape, 0) + place * width
+        pick = (lax.broadcasted_iota(jnp.int32, shape, 1) == wanted).astype(jnp.bfloat16)
+        cols_ref[part * width : (part + 1) * width, :] = lax.dot_general(
+            pick, states, ALONG, preferred_element_type=jnp.float32
+        )
+    projected_ref[...] = lax.dot_general(mine_ref[...], states, ALONG, preferred_element_type=jnp.float32)
+
+
+def load(mine, states, slot, width):
     count = states.shape[0]
     return pl.pallas_call(
         load_kernel,
         out_shape=(
-            jax.ShapeDtypeStruct((height, count), jnp.float32),
-            jax.ShapeDtypeStruct((width, count), jnp.float32),
+            jax.ShapeDtypeStruct((mine.shape[0], count), jnp.float32),
+            jax.ShapeDtypeStruct((2 * width, count), jnp.float32),
         ),
         in_specs=[SMEM, VMEM, VMEM],
         out_specs=(VMEM, VMEM),
         compiler_params=pltpu.CompilerParams(vmem_limit_bytes=LIMIT),
         name="load",
-    )(slot, flat, states)
+    )(slot, mine, states)
+
+
+def project_kernel(tensor_ref, states_ref, projected_ref):
+    projected_ref[...] = lax.dot_general(
+        tensor_ref[...], states_ref[...], ALONG, preferred_element_type=jnp.float32
+    )
+
+
+def project(flat, states):
+    return pl.pallas_call(
+        project_kernel,
+        out_shape=jax.ShapeDtypeStruct((flat.shape[0], states.shape[0]), jnp.float32),
+        in_specs=[VMEM, VMEM],
+        out_specs=VMEM,
+        compiler_params=pltpu.CompilerParams(vmem_limit_bytes=LIMIT),
+        name="project",
+    )(flat, states)
 
 
 def step_kernel(has_prev, keep_total, number, order, *refs):
-    slot_ref, low_ref, cols_ref, projected_ref, linear_ref, tensor_ref = refs[:6]
-    refs = refs[6:]
+    slot_ref, low_ref, cols_ref, own_ref, other_ref, linear_ref, mine_ref, swapped_ref = refs[:8]
+    refs = refs[8:]
     if has_prev:
         prev_ref, refs = refs[0], refs[1:]
     keep_ref, send_ref, refs = refs[0], refs[1], refs[2:]
@@ -179,49 +232,65 @@
         total_ref, refs = refs[0], refs[1:]
     (pair_ref,) = refs
     rows, batch = low_ref.shape
-    width = cols_ref.shape[0]
-    mine = slice(number * batch, (number + 1) * batch)
+    width = cols_ref.shape[0] // 2
+    height = rows * width
+    slot = slot_ref[0]
+    even = slot % 2 == 0
+    now = slice(number * batch, (number + 1) * batch)
     low = low_ref[...]
     low_float = low.astype(jnp.float32)
-    cols = cols_ref[:, mine]
-    first = jnp.dot(linear_ref[...], low, preferred_element_type=jnp.float32)
+    none = jnp.zeros((rows, batch), jnp.float32)
+    padded = jnp.concatenate([jnp.where(even, low_float, none), jnp.where(even, none, low_float)], 0)
+    lin = jnp.dot(linear_ref[...], padded.astype(jnp.bfloat16), preferred_element_type=jnp.float32)
+    lin_first, lin_last = lin[:width, :], lin[width:, :]
+    lins = (jnp.where(even, lin_first, lin_last), jnp.where(even, lin_last, lin_first))
     some = 128 // width
-    for c in range(rows // some):
-        part = low_float[c * some : (c + 1) * some, :]
-        spread = jnp.broadcast_to(part[:, None, :], (some, width, batch))
-        here = slice(c * 128, (c + 1) * 128)
-        pair = (spread * cols[None]).reshape(128, batch)
-        pair_ref[:, here] = pair.T.astype(jnp.bfloat16)
-        first = first + jnp.sum(spread * projected_ref[here, mine].reshape(some, width, batch), 0)
-    slot = slot_ref[0]
-    modes = tensor_ref.shape[1]
+    firsts = []
+    for part, projected_ref in enumerate((own_ref, other_ref)):
+        cols = cols_ref[part * width : (part + 1) * width, now]
+        first = lins[part]
+        for c in range(rows // some):
+            spread = jnp.broadcast_to(
+                low_float[c * some : (c + 1) * some, :][:, None, :], (some, width, batch)
+            )
+            here = slice(c * 128, (c + 1) * 128)
+            pair = (spread * cols[None]).reshape(128, batch)
+            pair_ref[:, part * height + c * 128 : part * height + (c + 1) * 128] = pair.T.astype(jnp.bfloat16)
+            first = first + jnp.sum(spread * projected_ref[here, now].reshape(some, width, batch), 0)
+        firsts.append(first)
+    extra = (jnp.where(even, firsts[0], firsts[1]), jnp.where(even, firsts[1], firsts[0]))
+    modes = mine_ref.shape[1]
     each = 256
-    pair = pair_ref[...]
+    pair_own, pair_other = pair_ref[:, :height], pair_ref[:, height:]
     for n in range(modes // each):
+        some_modes = pl.ds(n * each, each)
         second = jnp.dot(
-            pair, tensor_ref[:, n * each : (n + 1) * each], preferred_element_type=jnp.float32
-        ).T
+            pair_own, mine_ref[:, some_modes], preferred_element_type=jnp.float32
+        )
+        second = second + jnp.dot(
+            pair_other, swapped_ref[:, some_modes], preferred_element_type=jnp.float32
+        )
+        second = second.T
         for k in range(0, each // width, 2):
             block = (n * (each // width) + k) // 2
             halves = []
             for half in range(2):
                 piece = second[(k + half) * width : (k + half + 1) * width, :]
-                piece = piece + jnp.where(slot == 2 * block + half, first, 0.0)
+                piece = piece + jnp.where(slot // 2 == block, extra[half], 0.0)
                 if has_prev:
                     piece = piece + prev_ref[half, block]
                 if keep_total:
                     total_ref[half, block] = piece
                 halves.append(piece)
-            even = slot % 2 == 0
             keep_ref[order[block]] = jnp.where(even, halves[0], halves[1])
             send_ref[order[block]] = jnp.where(even, halves[1], halves[0]).astype(jnp.bfloat16)
 
 
-def step(flat, linear_t, projected, number, cols, low, slot, prev, keep_total, order):
-    modes = flat.shape[1]
-    width, batch = cols.shape[0], low.shape[1]
+def step(mine, swapped, linears, own, other, number, cols, low, slot, prev, keep_total, order):
+    modes = mine.shape[1]
+    width, batch = cols.shape[0] // 2, low.shape[1]
     full = (2, modes // (2 * width), width, batch)
-    args = [slot, low, cols, projected, linear_t, flat]
+    args = [slot, low, cols, own, other, linears, mine, swapped]
     if prev is not None:
         args.append(prev)
     shapes = [jax.ShapeDtypeStruct(full[1:], jnp.float32), jax.ShapeDtypeStruct(full[1:], jnp.bfloat16)]
@@ -232,7 +301,7 @@
         out_shape=shapes,
         in_specs=[SMEM] + [VMEM] * (len(args) - 1),
         out_specs=[VMEM] * len(shapes),
-        scratch_shapes=[pltpu.VMEM((batch, flat.shape[0]), jnp.bfloat16)],
+        scratch_shapes=[pltpu.VMEM((batch, 2 * mine.shape[0]), jnp.bfloat16)],
         compiler_params=pltpu.CompilerParams(vmem_limit_bytes=LIMIT),
         name="step",
     )(*args)
@@ -244,26 +313,30 @@
     slot = jnp.reshape(lax.axis_index(IN), (1,)).astype(jnp.int32)
     own = adjoint_end.T
     lam = start_rows(own)
-    flat = tensor.reshape(rows * width, modes)
-    projected, cols = load(flat, states.reshape(steps * batch, modes), slot, width)
+    mine, give = split(tensor.reshape(rows * width, modes), slot)
+    swapped = lax.ppermute(give, "core", [(0, 1), (1, 0)])
+    both_states = states.reshape(steps * batch, modes)
+    projected, cols = load(mine, both_states, slot, width)
+    linear, projected = lax.optimization_barrier((linear, projected))
+    linears = lax.all_gather(linear.T, "core").reshape(2 * width, rows)
+    other = project(swapped, both_states)
     order = range(16) if R1 == "A" else [b % 8 * 2 + b // 8 for b in range(16)]
     last = [b % 4 * 4 + b // 4 for b in range(16)]
     total = None
     for number in range(steps - 1, -1, -1):
-        low = lax.all_gather(lam.astype(jnp.bfloat16), "core").reshape(rows, batch)
         keep, send, *rest = step(
-            flat, linear.T, projected, number, cols, low, slot, total, number > 0, order if number else last
-        )
-        half = core_half(keep, send)
+            mine, swapped, linears, projected, other, number, cols, lam.astype(jnp.bfloat16), slot, total,
+            number > 0, order if number else last,
+        )
+        part = core_half(keep, send, slot)
         if number:
             total = rest[0]
-            lam = lam + step_size * to_out_blocks(half)
-    return (own + step_size * to_in_blocks(half)).T
+            lam = lam + step_size * to_out_blocks(part)
+    return (own + step_size * to_in_blocks(part)).T
 
 
 def solution(mesh):
     fine = Mesh(mesh.devices.reshape(SIZES), AXES)
     placed = (P(OUT, IN, None), P(OUT, IN), P(None, IN), P())
-    return jax.shard_map(
-        per_device, mesh=fine, in_specs=placed, out_specs=P(None, IN), check_vma=False
-    )
+
+    return jax.shard_map(per_device, mesh=fine, in_specs=placed, out_specs=P(None, IN), check_vma=False)

time: 90.9 us -> 92 us (1.012)
  starting transfers between devices: 11 us -> 12.8 us
  local copies, waits for them, and re-layouts: 3.24 us -> 2.2 us
    all_gather x2 -> x1, blocking collectives: 3.77 us -> 1.82 us  [per_device(): linears = lax.all_gather(linear.T, 'core').reshape(2 * width, rows)]
    ppermute x0 -> x1, starting transfers between devices: none -> 1.92 us  [per_device(): swapped = lax.ppermute(give, 'core', [(0, 1), (1, 0)])]
    all_to_all x4, blocking collectives: 63.8 us -> 65.6 us  [exchange(): return lax.all_to_all(pieces, axes, 0, 0, tiled=True)]
    unnamed x10 -> x8, local copies, waits for them, and re-layouts: 3.24 us -> 2.2 us
    pallas_call x1 -> x5, Pallas kernels: 1.47 us -> 2.14 us  [the longest x1 1.04 us: load(): pl.pallas_call(load_kernel, out_shape=(jax.ShapeDtypeStruct((mine.shape[0...]
  transfers between devices with their start and end apart: 1 -> 2, of which waited for: 0 -> 0; matrix products, arithmetic and copies ran while one was open for 0% -> 0% of each run, Pallas kernels for 2% -> 1%
where the time goes in v6:
time: 92 us; the launch traced here: 91.6 us
  blocking collectives  71.4 us (78%)
  starting transfers between devices  12.8 us (14%)
  Pallas kernels  4.4 us (5%)
  local copies, waits for them, and re-layouts  2.2 us (2%)
    all_to_all x4, blocking collectives, exchange(): return lax.all_to_all(pieces, axes, 0, 0, tiled=True)  65.6 us
    ppermute x1, starting transfers between devices, start_rows(): return lax.ppermute(own, AXES, perm)  10.9 us
    all_gather x2, blocking collectives, core_half(): both = lax.all_gather(send, 'core')  3.99 us
    pallas_call x2, Pallas kernels, step(): pl.pallas_call(functools.partial(step_kernel, prev is not None, keep_tota...  2.21 us
    unnamed x8, local copies, waits for them, and re-layouts  2.2 us
    ppermute x1, starting transfers between devices, per_device(): swapped = lax.ppermute(give, 'core', [(0, 1), (1, 0)])  1.92 us
  transfers between devices with their start and end apart: 2, of which 0 were waited for; matrix products, arithmetic and copies ran while one was open for 0% of the time, Pallas kernels for 1%

profile of v6, /device:TPU:8, one launch (start us, length us, event | category | flops | bytes accessed | tf_op | source)
XLA Modules:
  0.0 91.6 jit_solution(781726070105062306)
XLA Ops:
  0.0 0.0 copy-start
  0.0 2.2 %copy-done = bf16[64,32,1024]{2,1,0:T(8,128)(2,1)S(1)} copy-done((bf16[64,32,1024]{2,1,0:T(8,128)(2,1)S(1)}, bf16[64,32,1024]{2,1,0:T(8,128)(2,1)}, u32[]{:S(2)}) %copy-start) | copy-done | bytes 4194328
  2.2 0.0 copy-start.2
  2.2 0.0 copy-start.1
  2.2 0.3 split.1
  2.5 0.0 copy-start.3
  2.5 1.9 %collective-permute-start.1 = (bf16[1024,1024]{1,0:T(8,128)(2,1)S(1)}, bf16[1024,1024]{1,0:T(8,128)(2,1)S(1)}, u32[]{:S(2)}, u32[]{:S(2)}) collective-permute-start(bf16[1024,1024]{1,0:T(8,128)(2,1)S(1)} %get-tuple-element.20), channel_id=1, source_target_pairs={{0,1},{1,0},{2,3},{3,2},{4,5},{5,4},{6,7},{7,6},{8,9},{9,8},{10,11... | collective-permute-start | bytes 6291464 | tf_op jit(solution)/shard_map/ppermute | solution.py:317
  4.4 0.0 copy-done.2
  4.4 10.9 %collective-permute-start = (f32[32,128]{1,0:T(8,128)S(1)}, f32[32,128]{1,0:T(8,128)S(1)}, u32[]{:S(2)}, u32[]{:S(2)}) collective-permute-start(f32[32,128]{1,0:T(8,128)S(1)} %bitcast.22), channel_id=1, source_target_pairs={{0,12},{1,13},{32,10},{33,11},{64,8},{65,9},{96,2},{97,3},{128,0},... | collective-permute-start | bytes 49160 | tf_op jit(solution)/shard_map/ppermute | solution.py:90
  15.3 0.0 copy-done.1
  15.4 1.0 %load.1 = (f32[1024,256]{1,0:T(8,128)S(1)}, f32[64,256]{1,0:T(8,128)S(1)}) custom-call(s32[1]{0:T(128)} %bitcast.slot_ref.refs_0_, bf16[1024,1024]{1,0:T(8,128)(2,1)S(1)} %get-tuple-element.16.mine_ref.refs_6_, bf16[256,1024]{1,0:T(8,128)(2,1)S(1)} %bitcast.14), custom_call_target="tpu_custom_call" | custom-call | tf_op jit(solution)/shard_map/load/pallas_call | solution.py:195
  16.4 0.0 copy-done.3
  16.4 1.8 %all-gather.refs_5_ = bf16[64,64]{1,0:T(8,128)(2,1)S(1)} all-gather(bf16[32,64]{1,0:T(8,128)(2,1)S(1)} %bitcast.23), channel_id=2, replica_groups=mesh['yhi'=2,'z'=8,'ylo'=4,'x'=4,'core'=2] {'core'}, dimensions={0}, use_global_device_ids=true | all-gather | bytes 12288 | tf_op jit(solution)/shard_map/all_gather | solution.py:321
  18.2 0.0 collective-permute-done
  18.2 0.0 collective-permute-done.1.tensor_ref.refs_7_
  18.3 0.7 project.1.refs_4_
  19.0 1.1 %step.2 = (f32[16,32,128]{2,1,0:T(8,128)S(1)}, bf16[16,32,128]{2,1,0:T(8,128)(2,1)S(1)}, f32[2,16,32,128]{3,2,1,0:T(8,128)S(1)}) custom-call(s32[1]{0:T(128)} %bitcast.slot_ref.refs_0_, bf16[32,128]{1,0:T(8,128)(2,1)S(1)} %convert_element_type.12.refs_1_, f32[64,256]{1,0:T(8,128)S(1)} %get-tuple-element.17.refs_2_, ...), custom_call_target="tpu_custom_call" | custom-call | tf_op jit(solution)/shard_map/step/pallas_call | solution.py:299
  20.1 2.0 %all-gather.1 = bf16[32,32,128]{2,1,0:T(8,128)(2,1)S(1)} all-gather(bf16[16,32,128]{2,1,0:T(8,128)(2,1)S(1)} %get-tuple-element.23), channel_id=3, replica_groups=mesh['yhi'=2,'z'=8,'ylo'=4,'x'=4,'core'=2] {'core'}, dimensions={0}, use_global_device_ids=true | all-gather | bytes 393216 | tf_op jit(solution)/shard_map/all_gather | solution.py:100
  22.2 25.0 %all_to_all.20 = bf16[16,32,128]{2,1,0:T(8,128)(2,1)S(1)} all-to-all(bf16[16,32,128]{2,1,0:T(8,128)(2,1)S(1)} %join.2), channel_id=1, replica_groups=mesh['yhi'=2,'z'=8,'ylo'=4,'x'=4,'core'=2] {'yhi','z'}, dimensions={0} | all-to-all | bytes 262144 | tf_op jit(solution)/shard_map/all_to_all | solution.py:112
  47.2 13.2 %all_to_all.21 = bf16[16,32,128]{2,1,0:T(8,128)(2,1)S(1)} all-to-all(bf16[16,32,128]{2,1,0:T(8,128)(2,1)S(1)} %bitcast.19), channel_id=1, replica_groups=mesh['yhi'=2,'z'=8,'ylo'=4,'x'=4,'core'=2] {'x','ylo'}, dimensions={0} | all-to-all | bytes 262144 | tf_op jit(solution)/shard_map/all_to_all | solution.py:112
  60.4 1.1 %step.3 = (f32[16,32,128]{2,1,0:T(8,128)S(1)}, bf16[16,32,128]{2,1,0:T(8,128)(2,1)S(1)}) custom-call(s32[1]{0:T(128)} %bitcast.slot_ref.refs_0_, bf16[32,128]{1,0:T(8,128)(2,1)S(1)} %add_convert_fusion.refs_1_, f32[64,256]{1,0:T(8,128)S(1)} %get-tuple-element.17.refs_2_, f32[1024,256]{1,0:T(8,128)S(1)} %get-tuple-element.19.refs_3_, ...), custom_call_target="tpu_custom_call" | custom-call | tf_op jit(solution)/shard_map/step/pallas_call | solution.py:299
  61.5 2.0 %all-gather.2 = bf16[32,32,128]{2,1,0:T(8,128)(2,1)S(1)} all-gather(bf16[16,32,128]{2,1,0:T(8,128)(2,1)S(1)} %get-tuple-element.26), channel_id=4, replica_groups=mesh['yhi'=2,'z'=8,'ylo'=4,'x'=4,'core'=2] {'core'}, dimensions={0}, use_global_device_ids=true | all-gather | bytes 393216 | tf_op jit(solution)/shard_map/all_gather | solution.py:100
  63.6 11.2 %all_to_all.22 = bf16[16,32,128]{2,1,0:T(8,128)(2,1)S(1)} all-to-all(bf16[16,32,128]{2,1,0:T(8,128)(2,1)S(1)} %join.3), channel_id=1, replica_groups=mesh['yhi'=2,'z'=8,'ylo'=4,'x'=4,'core'=2] {'x','ylo'}, dimensions={0} | all-to-all | bytes 262144 | tf_op jit(solution)/shard_map/all_to_all | solution.py:112
  74.8 16.2 %all_to_all.23 = bf16[16,32,128]{2,1,0:T(8,128)(2,1)S(1)} all-to-all(bf16[16,32,128]{2,1,0:T(8,128)(2,1)S(1)} %bitcast.21), channel_id=1, replica_groups=mesh['yhi'=2,'z'=8,'ylo'=4,'x'=4,'core'=2] {'yhi','z'}, dimensions={0} | all-to-all | bytes 262144 | tf_op jit(solution)/shard_map/all_to_all | solution.py:112
  91.0 0.6 bitcast_add_fusion
  (8 shorter events, 0.2 us)
Async XLA Ops:
  0.0 2.2 %copy-start = (bf16[64,32,1024]{2,1,0:T(8,128)(2,1)S(1)}, bf16[64,32,1024]{2,1,0:T(8,128)(2,1)}, u32[]{:S(2)}) copy-start(bf16[64,32,1024]{2,1,0:T(8,128)(2,1)} %param.4) | copy-start | bytes 12582916
  2.2 2.2 %copy-start.2 = (f32[128,32]{0,1:T(8,128)S(1)}, f32[128,32]{0,1:T(8,128)}, u32[]{:S(2)}) copy-start(f32[128,32]{0,1:T(8,128)} %param.6) | copy-start | bytes 49156
  2.2 13.2 %copy-start.1 = (bf16[2,128,1024]{2,1,0:T(8,128)(2,1)S(1)}, bf16[2,128,1024]{2,1,0:T(8,128)(2,1)}, u32[]{:S(2)}) copy-start(bf16[2,128,1024]{2,1,0:T(8,128)(2,1)} %param.7) | copy-start | bytes 1572868
  2.5 13.9 %copy-start.3 = (bf16[64,32]{0,1:T(8,128)(2,1)S(1)}, bf16[64,32]{0,1:T(8,128)(2,1)}, u32[]{:S(2)}) copy-start(bf16[64,32]{0,1:T(8,128)(2,1)} %param.5) | copy-start | bytes 12292
  2.5 15.8 %collective-permute-start.1 = (bf16[1024,1024]{1,0:T(8,128)(2,1)S(1)}, bf16[1024,1024]{1,0:T(8,128)(2,1)S(1)}, u32[]{:S(2)}, u32[]{:S(2)}) collective-permute-start(bf16[1024,1024]{1,0:T(8,128)(2,1)S(1)} %get-tuple-element.20), channel_id=1, source_target_pairs={{0,1},{1,0},{2,3},{3,2},{4,5},{5,4},{6,7},{7,6},{8,9},{9,8},{10,11... | collective-permute-start | bytes 6291464 | tf_op jit(solution)/shard_map/ppermute | solution.py:317
  4.4 13.8 %collective-permute-start = (f32[32,128]{1,0:T(8,128)S(1)}, f32[32,128]{1,0:T(8,128)S(1)}, u32[]{:S(2)}, u32[]{:S(2)}) collective-permute-start(f32[32,128]{1,0:T(8,128)S(1)} %bitcast.22), channel_id=1, source_target_pairs={{0,12},{1,13},{32,10},{33,11},{64,8},{65,9},{96,2},{97,3},{128,0},... | collective-permute-start | bytes 49160 | tf_op jit(solution)/shard_map/ppermute | solution.py:90

commit v7 on v6

--- a/solution.py
+++ b/solution.py
@@ -49,7 +49,7 @@
 
 def assign(cost):
     n = len(cost)
-    weight = cost.astype(np.int64) ** 4
+    weight = 32 ** cost.astype(np.int64)
     row_of = [-1] * n
     high, low = [0] * (n + 1), [0] * (n + 1)
     match = [n] * (n + 1)
@@ -157,23 +157,29 @@
 ALONG = (((1,), (1,)), ((), ()))
 
 
-def split_kernel(slot_ref, tensor_ref, mine_ref, give_ref):
-    height = mine_ref.shape[0]
+def split_kernel(slot_ref, tensor_ref, linear_ref, mine_ref, give_ref):
+    width, rows = linear_ref.shape
+    height = tensor_ref.shape[0] // 2
     core = slot_ref[0] % 2
-    mine_ref[...] = tensor_ref[pl.ds(pl.multiple_of(core * height, height), height), :]
-    give_ref[...] = tensor_ref[pl.ds(pl.multiple_of((1 - core) * height, height), height), :]
-
-
-def split(flat, slot):
-    part = jax.ShapeDtypeStruct((flat.shape[0] // 2, flat.shape[1]), flat.dtype)
+    tail = slice(height, height + width)
+    for ref, part in ((mine_ref, core), (give_ref, 1 - core)):
+        ref[:height, :] = tensor_ref[pl.ds(pl.multiple_of(part * height, height), height), :]
+        ref[tail, :] = jnp.zeros((width, ref.shape[1]), ref.dtype)
+        ref[tail, : rows // 2] = jnp.where(
+            part == 0, linear_ref[:, : rows // 2].astype(jnp.float32), linear_ref[:, rows // 2 :].astype(jnp.float32)
+        ).astype(ref.dtype)
+
+
+def split(flat, linear_t, slot):
+    part = jax.ShapeDtypeStruct((flat.shape[0] // 2 + linear_t.shape[0], flat.shape[1]), flat.dtype)
     return pl.pallas_call(
         split_kernel,
         out_shape=(part, part),
-        in_specs=[SMEM, VMEM],
+        in_specs=[SMEM, VMEM, VMEM],
         out_specs=(VMEM, VMEM),
         compiler_params=pltpu.CompilerParams(vmem_limit_bytes=LIMIT),
         name="split",
-    )(slot, flat)
+    )(slot, flat, linear_t)
 
 
 def load_kernel(slot_ref, mine_ref, states_ref, projected_ref, cols_ref):
@@ -187,7 +193,8 @@
         cols_ref[part * width : (part + 1) * width, :] = lax.dot_general(
             pick, states, ALONG, preferred_element_type=jnp.float32
         )
-    projected_ref[...] = lax.dot_general(mine_ref[...], states, ALONG, preferred_element_type=jnp.float32)
+    rows = mine_ref[: projected_ref.shape[0], :]
+    projected_ref[...] = lax.dot_general(rows, states, ALONG, preferred_element_type=jnp.float32)
 
 
 def load(mine, states, slot, width):
@@ -195,7 +202,7 @@
     return pl.pallas_call(
         load_kernel,
         out_shape=(
-            jax.ShapeDtypeStruct((mine.shape[0], count), jnp.float32),
+            jax.ShapeDtypeStruct((mine.shape[0] - width, count), jnp.float32),
             jax.ShapeDtypeStruct((2 * width, count), jnp.float32),
         ),
         in_specs=[SMEM, VMEM, VMEM],
@@ -206,15 +213,14 @@
 
 
 def project_kernel(tensor_ref, states_ref, projected_ref):
-    projected_ref[...] = lax.dot_general(
-        tensor_ref[...], states_ref[...], ALONG, preferred_element_type=jnp.float32
-    )
-
-
-def project(flat, states):
+    rows = tensor_ref[: projected_ref.shape[0], :]
+    projected_ref[...] = lax.dot_general(rows, states_ref[...], ALONG, preferred_element_type=jnp.float32)
+
+
+def project(flat, states, width):
     return pl.pallas_call(
         project_kernel,
-        out_shape=jax.ShapeDtypeStruct((flat.shape[0], states.shape[0]), jnp.float32),
+        out_shape=jax.ShapeDtypeStruct((flat.shape[0] - width, states.shape[0]), jnp.float32),
         in_specs=[VMEM, VMEM],
         out_specs=VMEM,
         compiler_params=pltpu.CompilerParams(vmem_limit_bytes=LIMIT),
@@ -223,8 +229,8 @@
 
 
 def step_kernel(has_prev, keep_total, number, order, *refs):
-    slot_ref, low_ref, cols_ref, own_ref, other_ref, linear_ref, mine_ref, swapped_ref = refs[:8]
-    refs = refs[8:]
+    slot_ref, low_ref, cols_ref, own_ref, other_ref, mine_ref, swapped_ref = refs[:7]
+    refs = refs[7:]
     if has_prev:
         prev_ref, refs = refs[0], refs[1:]
     keep_ref, send_ref, refs = refs[0], refs[1], refs[2:]
@@ -239,11 +245,10 @@
     now = slice(number * batch, (number + 1) * batch)
     low = low_ref[...]
     low_float = low.astype(jnp.float32)
-    none = jnp.zeros((rows, batch), jnp.float32)
-    padded = jnp.concatenate([jnp.where(even, low_float, none), jnp.where(even, none, low_float)], 0)
-    lin = jnp.dot(linear_ref[...], padded.astype(jnp.bfloat16), preferred_element_type=jnp.float32)
-    lin_first, lin_last = lin[:width, :], lin[width:, :]
-    lins = (jnp.where(even, lin_first, lin_last), jnp.where(even, lin_last, lin_first))
+    tail = slice(height, height + width)
+    lins = [
+        jnp.dot(ref[tail, :rows], low, preferred_element_type=jnp.float32) for ref in (mine_ref, swapped_ref)
+    ]
     some = 128 // width
     firsts = []
     for part, projected_ref in enumerate((own_ref, other_ref)):
@@ -265,10 +270,10 @@
     for n in range(modes // each):
         some_modes = pl.ds(n * each, each)
         second = jnp.dot(
-            pair_own, mine_ref[:, some_modes], preferred_element_type=jnp.float32
+            pair_own, mine_ref[:height, some_modes], preferred_element_type=jnp.float32
         )
         second = second + jnp.dot(
-            pair_other, swapped_ref[:, some_modes], preferred_element_type=jnp.float32
+            pair_other, swapped_ref[:height, some_modes], preferred_element_type=jnp.float32
         )
         second = second.T
         for k in range(0, each // width, 2):
@@ -286,11 +291,11 @@
             send_ref[order[block]] = jnp.where(even, halves[1], halves[0]).astype(jnp.bfloat16)
 
 
-def step(mine, swapped, linears, own, other, number, cols, low, slot, prev, keep_total, order):
+def step(mine, swapped, own, other, number, cols, low, slot, prev, keep_total, order):
     modes = mine.shape[1]
     width, batch = cols.shape[0] // 2, low.shape[1]
     full = (2, modes // (2 * width), width, batch)
-    args = [slot, low, cols, own, other, linears, mine, swapped]
+    args = [slot, low, cols, own, other, mine, swapped]
     if prev is not None:
         args.append(prev)
     shapes = [jax.ShapeDtypeStruct(full[1:], jnp.float32), jax.ShapeDtypeStruct(full[1:], jnp.bfloat16)]
@@ -301,7 +306,7 @@
         out_shape=shapes,
         in_specs=[SMEM] + [VMEM] * (len(args) - 1),
         out_specs=[VMEM] * len(shapes),
-        scratch_shapes=[pltpu.VMEM((batch, 2 * mine.shape[0]), jnp.bfloat16)],
+        scratch_shapes=[pltpu.VMEM((batch, 2 * own.shape[0]), jnp.bfloat16)],
         compiler_params=pltpu.CompilerParams(vmem_limit_bytes=LIMIT),
         name="step",
     )(*args)
@@ -313,19 +318,17 @@
     slot = jnp.reshape(lax.axis_index(IN), (1,)).astype(jnp.int32)
     own = adjoint_end.T
     lam = start_rows(own)
-    mine, give = split(tensor.reshape(rows * width, modes), slot)
+    mine, give = split(tensor.reshape(rows * width, modes), linear.T, slot)
     swapped = lax.ppermute(give, "core", [(0, 1), (1, 0)])
     both_states = states.reshape(steps * batch, modes)
     projected, cols = load(mine, both_states, slot, width)
-    linear, projected = lax.optimization_barrier((linear, projected))
-    linears = lax.all_gather(linear.T, "core").reshape(2 * width, rows)
-    other = project(swapped, both_states)
+    other = project(swapped, both_states, width)
     order = range(16) if R1 == "A" else [b % 8 * 2 + b // 8 for b in range(16)]
     last = [b % 4 * 4 + b // 4 for b in range(16)]
     total = None
     for number in range(steps - 1, -1, -1):
         keep, send, *rest = step(
-            mine, swapped, linears, projected, other, number, cols, lam.astype(jnp.bfloat16), slot, total,
+            mine, swapped, projected, other, number, cols, lam.astype(jnp.bfloat16), slot, total,
             number > 0, order if number else last,
         )
         part = core_half(keep, send, slot)

time: 92 us -> 92.7 us (level)
    all_gather x1 -> x0, blocking collectives: 1.82 us -> none  [per_device(): linears = lax.all_gather(linear.T, 'core').reshape(2 * width, rows)]
    all_to_all x4, blocking collectives: 65.6 us -> 67.1 us  [exchange(): return lax.all_to_all(pieces, axes, 0, 0, tiled=True)]
  transfers between devices with their start and end apart: 2 -> 2, of which waited for: 0 -> 1; matrix products, arithmetic and copies ran while one was open for 0% -> 0% of each run, Pallas kernels for 1% -> 1%
where the time goes in v7:
time: 92.7 us; the launch traced here: 92.3 us
  blocking collectives  71 us (77%)
  starting transfers between devices  12.8 us (14%)
  Pallas kernels  4.39 us (5%)
  local copies, waits for them, and re-layouts  2.9 us (3%)
    all_to_all x4, blocking collectives, exchange(): return lax.all_to_all(pieces, axes, 0, 0, tiled=True)  67.1 us
    ppermute x1, starting transfers between devices, start_rows(): return lax.ppermute(own, AXES, perm)  10.9 us
    all_gather x2, blocking collectives, core_half(): both = lax.all_gather(send, 'core')  3.99 us
    unnamed x8, local copies, waits for them, and re-layouts  2.9 us
    pallas_call x2, Pallas kernels, step(): pl.pallas_call(functools.partial(step_kernel, prev is not None, keep_tota...  2.18 us
    ppermute x1, starting transfers between devices, per_device(): swapped = lax.ppermute(give, 'core', [(0, 1), (1, 0)])  1.92 us
  transfers between devices with their start and end apart: 2, of which 1 were waited for; matrix products, arithmetic and copies ran while one was open for 0% of the time, Pallas kernels for 1%

profile of v7, /device:TPU:8, one launch (start us, length us, event | category | flops | bytes accessed | tf_op | source)
XLA Modules:
  0.0 92.3 jit_solution(16999034161229799388)
XLA Ops:
  0.0 0.0 copy-start.3
  0.0 0.0 copy-start
  0.0 2.2 %copy-done = bf16[64,32,1024]{2,1,0:T(8,128)(2,1)S(1)} copy-done((bf16[64,32,1024]{2,1,0:T(8,128)(2,1)S(1)}, bf16[64,32,1024]{2,1,0:T(8,128)(2,1)}, u32[]{:S(2)}) %copy-start) | copy-done | bytes 4194328
  2.2 0.0 copy-start.2
  2.2 0.7 copy-done.2
  2.9 0.0 copy-start.1
  2.9 0.3 split.1
  3.2 1.9 %collective-permute-start.1 = (bf16[1056,1024]{1,0:T(8,128)(2,1)S(1)}, bf16[1056,1024]{1,0:T(8,128)(2,1)S(1)}, u32[]{:S(2)}, u32[]{:S(2)}) collective-permute-start(bf16[1056,1024]{1,0:T(8,128)(2,1)S(1)} %get-tuple-element.17), channel_id=1, source_target_pairs={{0,1},{1,0},{2,3},{3,2},{4,5},{5,4},{6,7},{7,6},{8,9},{9,8},{10,11... | collective-permute-start | bytes 6488072 | tf_op jit(solution)/shard_map/ppermute | solution.py:322
  5.1 0.0 copy-done.3
  5.1 10.9 %collective-permute-start = (f32[32,128]{1,0:T(8,128)S(1)}, f32[32,128]{1,0:T(8,128)S(1)}, u32[]{:S(2)}, u32[]{:S(2)}) collective-permute-start(f32[32,128]{1,0:T(8,128)S(1)} %bitcast.23), channel_id=1, source_target_pairs={{0,12},{1,13},{32,10},{33,11},{64,8},{65,9},{96,2},{97,3},{128,0},... | collective-permute-start | bytes 49160 | tf_op jit(solution)/shard_map/ppermute | solution.py:90
  16.1 0.0 copy-done.1
  16.1 1.0 %load.1 = (f32[1024,256]{1,0:T(8,128)S(1)}, f32[64,256]{1,0:T(8,128)S(1)}) custom-call(s32[1]{0:T(128)} %bitcast.slot_ref.refs_0_, bf16[1056,1024]{1,0:T(8,128)(2,1)S(1)} %get-tuple-element.14.mine_ref.refs_5_, bf16[256,1024]{1,0:T(8,128)(2,1)S(1)} %bitcast.14), custom_call_target="tpu_custom_call" | custom-call | tf_op jit(solution)/shard_map/load/pallas_call | solution.py:202
  17.1 0.4 collective-permute-done
  17.5 0.0 collective-permute-done.1.tensor_ref.refs_6_
  17.5 0.7 project.1.refs_4_
  18.2 1.1 %step.2 = (f32[16,32,128]{2,1,0:T(8,128)S(1)}, bf16[16,32,128]{2,1,0:T(8,128)(2,1)S(1)}, f32[2,16,32,128]{3,2,1,0:T(8,128)S(1)}) custom-call(s32[1]{0:T(128)} %bitcast.slot_ref.refs_0_, bf16[32,128]{1,0:T(8,128)(2,1)S(1)} %convert_element_type.12.refs_1_, f32[64,256]{1,0:T(8,128)S(1)} %get-tuple-element.15.refs_2_, ...), custom_call_target="tpu_custom_call" | custom-call | tf_op jit(solution)/shard_map/step/pallas_call | solution.py:304
  19.3 2.0 %all-gather = bf16[32,32,128]{2,1,0:T(8,128)(2,1)S(1)} all-gather(bf16[16,32,128]{2,1,0:T(8,128)(2,1)S(1)} %get-tuple-element.19), channel_id=2, replica_groups=mesh['yhi'=2,'z'=8,'ylo'=4,'x'=4,'core'=2] {'core'}, dimensions={0}, use_global_device_ids=true | all-gather | bytes 393216 | tf_op jit(solution)/shard_map/all_gather | solution.py:100
  21.4 26.5 %all_to_all.20 = bf16[16,32,128]{2,1,0:T(8,128)(2,1)S(1)} all-to-all(bf16[16,32,128]{2,1,0:T(8,128)(2,1)S(1)} %join.2), channel_id=1, replica_groups=mesh['yhi'=2,'z'=8,'ylo'=4,'x'=4,'core'=2] {'yhi','z'}, dimensions={0} | all-to-all | bytes 262144 | tf_op jit(solution)/shard_map/all_to_all | solution.py:112
  47.9 13.2 %all_to_all.21 = bf16[16,32,128]{2,1,0:T(8,128)(2,1)S(1)} all-to-all(bf16[16,32,128]{2,1,0:T(8,128)(2,1)S(1)} %bitcast.19), channel_id=1, replica_groups=mesh['yhi'=2,'z'=8,'ylo'=4,'x'=4,'core'=2] {'x','ylo'}, dimensions={0} | all-to-all | bytes 262144 | tf_op jit(solution)/shard_map/all_to_all | solution.py:112
  61.1 1.1 %step.3 = (f32[16,32,128]{2,1,0:T(8,128)S(1)}, bf16[16,32,128]{2,1,0:T(8,128)(2,1)S(1)}) custom-call(s32[1]{0:T(128)} %bitcast.slot_ref.refs_0_, bf16[32,128]{1,0:T(8,128)(2,1)S(1)} %add_convert_fusion.refs_1_, f32[64,256]{1,0:T(8,128)S(1)} %get-tuple-element.15.refs_2_, f32[1024,256]{1,0:T(8,128)S(1)} %get-tuple-element.16.refs_3_, ...), custom_call_target="tpu_custom_call" | custom-call | tf_op jit(solution)/shard_map/step/pallas_call | solution.py:304
  62.2 2.0 %all-gather.1 = bf16[32,32,128]{2,1,0:T(8,128)(2,1)S(1)} all-gather(bf16[16,32,128]{2,1,0:T(8,128)(2,1)S(1)} %get-tuple-element.22), channel_id=3, replica_groups=mesh['yhi'=2,'z'=8,'ylo'=4,'x'=4,'core'=2] {'core'}, dimensions={0}, use_global_device_ids=true | all-gather | bytes 393216 | tf_op jit(solution)/shard_map/all_gather | solution.py:100
  64.2 11.2 %all_to_all.22 = bf16[16,32,128]{2,1,0:T(8,128)(2,1)S(1)} all-to-all(bf16[16,32,128]{2,1,0:T(8,128)(2,1)S(1)} %join.3), channel_id=1, replica_groups=mesh['yhi'=2,'z'=8,'ylo'=4,'x'=4,'core'=2] {'x','ylo'}, dimensions={0} | all-to-all | bytes 262144 | tf_op jit(solution)/shard_map/all_to_all | solution.py:112
  75.5 16.2 %all_to_all.23 = bf16[16,32,128]{2,1,0:T(8,128)(2,1)S(1)} all-to-all(bf16[16,32,128]{2,1,0:T(8,128)(2,1)S(1)} %bitcast.21), channel_id=1, replica_groups=mesh['yhi'=2,'z'=8,'ylo'=4,'x'=4,'core'=2] {'yhi','z'}, dimensions={0} | all-to-all | bytes 262144 | tf_op jit(solution)/shard_map/all_to_all | solution.py:112
  91.7 0.6 bitcast_add_fusion
  (8 shorter events, 0.2 us)
Async XLA Ops:
  0.0 5.1 %copy-start.3 = (f32[128,32]{0,1:T(8,128)S(1)}, f32[128,32]{0,1:T(8,128)}, u32[]{:S(2)}) copy-start(f32[128,32]{0,1:T(8,128)} %param.6) | copy-start | bytes 49156
  0.0 2.2 %copy-start = (bf16[64,32,1024]{2,1,0:T(8,128)(2,1)S(1)}, bf16[64,32,1024]{2,1,0:T(8,128)(2,1)}, u32[]{:S(2)}) copy-start(bf16[64,32,1024]{2,1,0:T(8,128)(2,1)} %param.4) | copy-start | bytes 12582916
  2.2 0.7 copy-start.2
  2.9 13.2 %copy-start.1 = (bf16[2,128,1024]{2,1,0:T(8,128)(2,1)S(1)}, bf16[2,128,1024]{2,1,0:T(8,128)(2,1)}, u32[]{:S(2)}) copy-start(bf16[2,128,1024]{2,1,0:T(8,128)(2,1)} %param.7) | copy-start | bytes 1572868
  3.2 14.3 %collective-permute-start.1 = (bf16[1056,1024]{1,0:T(8,128)(2,1)S(1)}, bf16[1056,1024]{1,0:T(8,128)(2,1)S(1)}, u32[]{:S(2)}, u32[]{:S(2)}) collective-permute-start(bf16[1056,1024]{1,0:T(8,128)(2,1)S(1)} %get-tuple-element.17), channel_id=1, source_target_pairs={{0,1},{1,0},{2,3},{3,2},{4,5},{5,4},{6,7},{7,6},{8,9},{9,8},{10,11... | collective-permute-start | bytes 6488072 | tf_op jit(solution)/shard_map/ppermute | solution.py:322
  5.1 12.3 %collective-permute-start = (f32[32,128]{1,0:T(8,128)S(1)}, f32[32,128]{1,0:T(8,128)S(1)}, u32[]{:S(2)}, u32[]{:S(2)}) collective-permute-start(f32[32,128]{1,0:T(8,128)S(1)} %bitcast.23), channel_id=1, source_target_pairs={{0,12},{1,13},{32,10},{33,11},{64,8},{65,9},{96,2},{97,3},{128,0},... | collective-permute-start | bytes 49160 | tf_op jit(solution)/shard_map/ppermute | solution.py:90

commit v8 on v6

--- a/solution.py
+++ b/solution.py
@@ -13,6 +13,8 @@
 VMEM = pl.BlockSpec(memory_space=pltpu.VMEM)
 SMEM = pl.BlockSpec(memory_space=pltpu.SMEM)
 LIMIT = 16 * 1024 * 1024
+LOAD_LIMIT = 48 * 1024 * 1024
+CHUNKS = 4
 AXES = ("yhi", "z", "ylo", "x", "core")
 SIZES = (2, 8, 4, 4, 2)
 OUT = ("yhi", "z")
@@ -90,22 +92,45 @@
     return lax.ppermute(own, AXES, perm)
 
 
-def join_kernel(slot_ref, keep_ref, both_ref, half_ref):
-    even = slot_ref[0] % 2 == 0
-    got = jnp.where(even, both_ref[1].astype(jnp.float32), both_ref[0].astype(jnp.float32))
-    half_ref[...] = (keep_ref[...] + got).astype(jnp.bfloat16)
-
-
-def core_half(keep, send, slot):
+def quadrant(linear_ref, first):
+    rows = linear_ref.shape[1] // 2
+    left, right = linear_ref[:, :rows].astype(jnp.float32), linear_ref[:, rows:].astype(jnp.float32)
+    return jnp.where(first, left, right).astype(jnp.bfloat16)
+
+
+def join_kernel(has_prev, order, slot_ref, keep_ref, both_ref, linear_ref, *refs):
+    half_ref, rest_ref = refs[-2:]
+    slot = slot_ref[0]
+    even = slot % 2 == 0
+    blocks = keep_ref.shape[0]
+    low = jnp.where(even, both_ref[1, blocks].astype(jnp.float32), both_ref[0, blocks].astype(jnp.float32))
+    rest = jnp.dot(
+        quadrant(linear_ref, ~even), low.astype(jnp.bfloat16), preferred_element_type=jnp.float32
+    )
+    if has_prev:
+        rest = rest + refs[0][...]
+    rest_ref[...] = rest
+    for block in range(blocks):
+        at = order[block]
+        got = jnp.where(even, both_ref[1, at].astype(jnp.float32), both_ref[0, at].astype(jnp.float32))
+        here = jnp.where(slot // 2 == block, rest, 0.0)
+        half_ref[at] = (keep_ref[at] + got + here).astype(jnp.bfloat16)
+
+
+def core_half(keep, send, slot, linear_t, prev, order):
     both = lax.all_gather(send, "core")
-    return pl.pallas_call(
-        join_kernel,
-        out_shape=jax.ShapeDtypeStruct(keep.shape, jnp.bfloat16),
-        in_specs=[SMEM, VMEM, VMEM],
-        out_specs=VMEM,
+    args = [slot, keep, both, linear_t] + ([] if prev is None else [prev])
+    return pl.pallas_call(
+        functools.partial(join_kernel, prev is not None, tuple(order)),
+        out_shape=(
+            jax.ShapeDtypeStruct(keep.shape, jnp.bfloat16),
+            jax.ShapeDtypeStruct(keep.shape[1:], jnp.float32),
+        ),
+        in_specs=[SMEM] + [VMEM] * (len(args) - 1),
+        out_specs=(VMEM, VMEM),
         compiler_params=pltpu.CompilerParams(vmem_limit_bytes=LIMIT),
         name="join",
-    )(slot, keep, both)
+    )(*args)
 
 
 def exchange(pieces, axes):
@@ -157,29 +182,41 @@
 ALONG = (((1,), (1,)), ((), ()))
 
 
-def split_kernel(slot_ref, tensor_ref, mine_ref, give_ref):
-    height = mine_ref.shape[0]
-    core = slot_ref[0] % 2
-    mine_ref[...] = tensor_ref[pl.ds(pl.multiple_of(core * height, height), height), :]
-    give_ref[...] = tensor_ref[pl.ds(pl.multiple_of((1 - core) * height, height), height), :]
+def split_kernel(slot_ref, tensor_ref, give_ref, sem):
+    height = give_ref.shape[0]
+    start = pl.multiple_of((1 - slot_ref[0] % 2) * height, height)
+    copy = pltpu.make_async_copy(tensor_ref.at[pl.ds(start, height)], give_ref, sem)
+    copy.start()
+    copy.wait()
 
 
 def split(flat, slot):
-    part = jax.ShapeDtypeStruct((flat.shape[0] // 2, flat.shape[1]), flat.dtype)
     return pl.pallas_call(
         split_kernel,
-        out_shape=(part, part),
-        in_specs=[SMEM, VMEM],
-        out_specs=(VMEM, VMEM),
-        compiler_params=pltpu.CompilerParams(vmem_limit_bytes=LIMIT),
+        out_shape=jax.ShapeDtypeStruct((flat.shape[0] // 2, flat.shape[1]), flat.dtype),
+        in_specs=[SMEM, pl.BlockSpec(memory_space=pl.ANY)],
+        out_specs=VMEM,
+        scratch_shapes=[pltpu.SemaphoreType.DMA],
+        compiler_params=pltpu.CompilerParams(vmem_limit_bytes=LOAD_LIMIT),
         name="split",
     )(slot, flat)
 
 
-def load_kernel(slot_ref, mine_ref, states_ref, projected_ref, cols_ref):
+def load_kernel(slot_ref, tensor_ref, states_ref, mine_ref, projected_ref, cols_ref, sems):
+    slot = slot_ref[0]
+    height = mine_ref.shape[0]
+    each = height // CHUNKS
+    copies = []
+    for c in range(CHUNKS):
+        start = pl.multiple_of(slot % 2 * height + c * each, each)
+        copies.append(
+            pltpu.make_async_copy(
+                tensor_ref.at[pl.ds(start, each)], mine_ref.at[pl.ds(c * each, each)], sems.at[c]
+            )
+        )
+        copies[-1].start()
     states = states_ref[...]
     width = cols_ref.shape[0] // 2
-    slot = slot_ref[0]
     shape = (width, states.shape[1])
     for part, place in enumerate((slot, slot + 1 - 2 * (slot % 2))):
         wanted = lax.broadcasted_iota(jnp.int32, shape, 0) + place * width
@@ -187,22 +224,30 @@
         cols_ref[part * width : (part + 1) * width, :] = lax.dot_general(
             pick, states, ALONG, preferred_element_type=jnp.float32
         )
-    projected_ref[...] = lax.dot_general(mine_ref[...], states, ALONG, preferred_element_type=jnp.float32)
-
-
-def load(mine, states, slot, width):
+    for c in range(CHUNKS):
+        copies[c].wait()
+        rows = slice(c * each, (c + 1) * each)
+        projected_ref[rows, :] = lax.dot_general(
+            mine_ref[rows, :], states, ALONG, preferred_element_type=jnp.float32
+        )
+
+
+def load(flat, states, slot, width):
     count = states.shape[0]
+    half = flat.shape[0] // 2
     return pl.pallas_call(
         load_kernel,
         out_shape=(
-            jax.ShapeDtypeStruct((mine.shape[0], count), jnp.float32),
+            jax.ShapeDtypeStruct((half, flat.shape[1]), flat.dtype),
+            jax.ShapeDtypeStruct((half, count), jnp.float32),
             jax.ShapeDtypeStruct((2 * width, count), jnp.float32),
         ),
-        in_specs=[SMEM, VMEM, VMEM],
-        out_specs=(VMEM, VMEM),
-        compiler_params=pltpu.CompilerParams(vmem_limit_bytes=LIMIT),
+        in_specs=[SMEM, pl.BlockSpec(memory_space=pl.ANY), VMEM],
+        out_specs=(VMEM, VMEM, VMEM),
+        scratch_shapes=[pltpu.SemaphoreType.DMA((CHUNKS,))],
+        compiler_params=pltpu.CompilerParams(vmem_limit_bytes=LOAD_LIMIT),
         name="load",
-    )(slot, mine, states)
+    )(slot, flat, states)
 
 
 def project_kernel(tensor_ref, states_ref, projected_ref):
@@ -239,11 +284,8 @@
     now = slice(number * batch, (number + 1) * batch)
     low = low_ref[...]
     low_float = low.astype(jnp.float32)
-    none = jnp.zeros((rows, batch), jnp.float32)
-    padded = jnp.concatenate([jnp.where(even, low_float, none), jnp.where(even, none, low_float)], 0)
-    lin = jnp.dot(linear_ref[...], padded.astype(jnp.bfloat16), preferred_element_type=jnp.float32)
-    lin_first, lin_last = lin[:width, :], lin[width:, :]
-    lins = (jnp.where(even, lin_first, lin_last), jnp.where(even, lin_last, lin_first))
+    lin = jnp.dot(quadrant(linear_ref, even), low, preferred_element_type=jnp.float32)
+    lins = (lin, jnp.zeros_like(lin))
     some = 128 // width
     firsts = []
     for part, projected_ref in enumerate((own_ref, other_ref)):
@@ -284,6 +326,7 @@
                 halves.append(piece)
             keep_ref[order[block]] = jnp.where(even, halves[0], halves[1])
             send_ref[order[block]] = jnp.where(even, halves[1], halves[0]).astype(jnp.bfloat16)
+    send_ref[keep_ref.shape[0]] = low
 
 
 def step(mine, swapped, linears, own, other, number, cols, low, slot, prev, keep_total, order):
@@ -293,7 +336,8 @@
     args = [slot, low, cols, own, other, linears, mine, swapped]
     if prev is not None:
         args.append(prev)
-    shapes = [jax.ShapeDtypeStruct(full[1:], jnp.float32), jax.ShapeDtypeStruct(full[1:], jnp.bfloat16)]
+    shapes = [jax.ShapeDtypeStruct(full[1:], jnp.float32)]
+    shapes.append(jax.ShapeDtypeStruct((full[1] + 1,) + full[2:], jnp.bfloat16))
     if keep_total:
         shapes.append(jax.ShapeDtypeStruct(full, jnp.float32))
     return pl.pallas_call(
@@ -313,22 +357,22 @@
     slot = jnp.reshape(lax.axis_index(IN), (1,)).astype(jnp.int32)
     own = adjoint_end.T
     lam = start_rows(own)
-    mine, give = split(tensor.reshape(rows * width, modes), slot)
+    flat = tensor.reshape(rows * width, modes)
+    give = split(flat, slot)
     swapped = lax.ppermute(give, "core", [(0, 1), (1, 0)])
     both_states = states.reshape(steps * batch, modes)
-    projected, cols = load(mine, both_states, slot, width)
-    linear, projected = lax.optimization_barrier((linear, projected))
-    linears = lax.all_gather(linear.T, "core").reshape(2 * width, rows)
+    mine, projected, cols = load(flat, both_states, slot, width)
+    linear_t = linear.T
     other = project(swapped, both_states)
     order = range(16) if R1 == "A" else [b % 8 * 2 + b // 8 for b in range(16)]
     last = [b % 4 * 4 + b // 4 for b in range(16)]
-    total = None
+    total = rest_lin = None
     for number in range(steps - 1, -1, -1):
         keep, send, *rest = step(
-            mine, swapped, linears, projected, other, number, cols, lam.astype(jnp.bfloat16), slot, total,
+            mine, swapped, linear_t, projected, other, number, cols, lam.astype(jnp.bfloat16), slot, total,
             number > 0, order if number else last,
         )
-        part = core_half(keep, send, slot)
+        part, rest_lin = core_half(keep, send, slot, linear_t, rest_lin, order if number else last)
         if number:
             total = rest[0]
             lam = lam + step_size * to_out_blocks(part)

time: 92 us -> 92.2 us (level)
  Pallas kernels: 4.4 us -> 8.88 us
  local copies, waits for them, and re-layouts: 2.2 us -> 0.01 us
  blocking collectives: 71.4 us -> 69.3 us
    pallas_call x4, Pallas kernels: 1.4 us -> 5.98 us  [the longest x1 3.17 us: load(): pl.pallas_call(load_kernel, out_shape=(jax.ShapeDtypeStruct((half, flat.s...]
    unnamed x8 -> x6, local copies, waits for them, and re-layouts: 2.2 us -> 0.01 us
    all_gather x1 -> x0, blocking collectives: 1.82 us -> none  [per_device(): linears = lax.all_gather(linear.T, 'core').reshape(2 * width, rows)]
  transfers between devices with their start and end apart: 2 -> 2, of which waited for: 0 -> 0; matrix products, arithmetic and copies ran while one was open for 0% -> 0% of each run, Pallas kernels for 1% -> 3%
where the time goes in v8:
time: 92.2 us; the launch traced here: 91.8 us
  blocking collectives  69.3 us (75%)
  starting transfers between devices  12.8 us (14%)
  Pallas kernels  8.88 us (10%)
    all_to_all x4, blocking collectives, exchange(): return lax.all_to_all(pieces, axes, 0, 0, tiled=True)  65.2 us
    ppermute x1, starting transfers between devices, start_rows(): return lax.ppermute(own, AXES, perm)  10.9 us
    all_gather x2, blocking collectives, core_half(): both = lax.all_gather(send, 'core')  4.01 us
    pallas_call x1, Pallas kernels, load(): pl.pallas_call(load_kernel, out_shape=(jax.ShapeDtypeStruct((half, flat.s...  3.17 us
    pallas_call x2, Pallas kernels, step(): pl.pallas_call(functools.partial(step_kernel, prev is not None, keep_tota...  2.1 us
    ppermute x1, starting transfers between devices, per_device(): swapped = lax.ppermute(give, 'core', [(0, 1), (1, 0)])  1.92 us
  transfers between devices with their start and end apart: 2, of which 0 were waited for; matrix products, arithmetic and copies ran while one was open for 0% of the time, Pallas kernels for 3%

profile of v8, /device:TPU:8, one launch (start us, length us, event | category | flops | bytes accessed | tf_op | source)
XLA Modules:
  0.0 91.8 jit_solution(7725569533835597054)
XLA Ops:
  0.0 0.0 copy-start.2
  0.0 0.0 copy-start
  0.0 1.7 %split.1 = bf16[1024,1024]{1,0:T(8,128)(2,1)S(1)} custom-call(s32[1]{0:T(128)} %bitcast.slot_ref.refs_0_, bf16[2048,1024]{1,0:T(8,128)(2,1)} %bitcast.25), custom_call_target="tpu_custom_call" | custom-call | tf_op jit(solution)/shard_map/split/pallas_call | solution.py:194
  1.7 1.9 %collective-permute-start.1 = (bf16[1024,1024]{1,0:T(8,128)(2,1)S(1)}, bf16[1024,1024]{1,0:T(8,128)(2,1)S(1)}, u32[]{:S(2)}, u32[]{:S(2)}) collective-permute-start(bf16[1024,1024]{1,0:T(8,128)(2,1)S(1)} %split.1), channel_id=1, source_target_pairs={{0,1},{1,0},{2,3},{3,2},{4,5},{5,4},{6,7},{7,6},{8,9},{9,8},{10,11... | collective-permute-start | bytes 6291464 | tf_op jit(solution)/shard_map/ppermute | solution.py:362
  3.6 0.0 copy-done.2
  3.6 10.9 %collective-permute-start = (f32[32,128]{1,0:T(8,128)S(1)}, f32[32,128]{1,0:T(8,128)S(1)}, u32[]{:S(2)}, u32[]{:S(2)}) collective-permute-start(f32[32,128]{1,0:T(8,128)S(1)} %bitcast.27), channel_id=1, source_target_pairs={{0,12},{1,13},{32,10},{33,11},{64,8},{65,9},{96,2},{97,3},{128,0},... | collective-permute-start | bytes 49160 | tf_op jit(solution)/shard_map/ppermute | solution.py:92
  14.5 0.0 copy-done
  14.5 3.2 %load.1 = (bf16[1024,1024]{1,0:T(8,128)(2,1)S(1)}, f32[1024,256]{1,0:T(8,128)S(1)}, f32[64,256]{1,0:T(8,128)S(1)}) custom-call(s32[1]{0:T(128)} %bitcast.slot_ref.refs_0_, bf16[2048,1024]{1,0:T(8,128)(2,1)} %bitcast.26, bf16[256,1024]{1,0:T(8,128)(2,1)S(1)} %bitcast.13), custom_call_target="tpu_custom_call" | custom-call | tf_op jit(solution)/shard_map/load/pallas_call | solution.py:238
  17.7 0.0 copy-start.1
  17.7 0.0 collective-permute-done
  17.8 0.0 collective-permute-done.1.tensor_ref.refs_7_
  17.8 0.7 project.1.refs_4_
  18.5 0.0 copy-done.1
  18.5 1.1 %step.2 = (f32[16,32,128]{2,1,0:T(8,128)S(1)}, bf16[17,32,128]{2,1,0:T(8,128)(2,1)S(1)}, f32[2,16,32,128]{3,2,1,0:T(8,128)S(1)}) custom-call(s32[1]{0:T(128)} %bitcast.slot_ref.refs_0_, bf16[32,128]{1,0:T(8,128)(2,1)S(1)} %convert_element_type.12.refs_1_, f32[64,256]{1,0:T(8,128)S(1)} %get-tuple-element.16.refs_2_, ...), custom_call_target="tpu_custom_call" | custom-call | tf_op jit(solution)/shard_map/step/pallas_call | solution.py:343
  19.6 2.0 %all-gather = bf16[34,32,128]{2,1,0:T(8,128)(2,1)S(1)} all-gather(bf16[17,32,128]{2,1,0:T(8,128)(2,1)S(1)} %get-tuple-element.20), channel_id=2, replica_groups=mesh['yhi'=2,'z'=8,'ylo'=4,'x'=4,'core'=2] {'core'}, dimensions={0}, use_global_device_ids=true | all-gather | bytes 417792 | tf_op jit(solution)/shard_map/all_gather | solution.py:121
  21.6 0.3 join.2
  21.9 24.7 %all_to_all.20 = bf16[16,32,128]{2,1,0:T(8,128)(2,1)S(1)} all-to-all(bf16[16,32,128]{2,1,0:T(8,128)(2,1)S(1)} %get-tuple-element.21), channel_id=1, replica_groups=mesh['yhi'=2,'z'=8,'ylo'=4,'x'=4,'core'=2] {'yhi','z'}, dimensions={0} | all-to-all | bytes 262144 | tf_op jit(solution)/shard_map/all_to_all | solution.py:137
  46.6 13.2 %all_to_all.21 = bf16[16,32,128]{2,1,0:T(8,128)(2,1)S(1)} all-to-all(bf16[16,32,128]{2,1,0:T(8,128)(2,1)S(1)} %bitcast.18), channel_id=1, replica_groups=mesh['yhi'=2,'z'=8,'ylo'=4,'x'=4,'core'=2] {'x','ylo'}, dimensions={0} | all-to-all | bytes 262144 | tf_op jit(solution)/shard_map/all_to_all | solution.py:137
  59.8 1.1 %step.3 = (f32[16,32,128]{2,1,0:T(8,128)S(1)}, bf16[17,32,128]{2,1,0:T(8,128)(2,1)S(1)}) custom-call(s32[1]{0:T(128)} %bitcast.slot_ref.refs_0_, bf16[32,128]{1,0:T(8,128)(2,1)S(1)} %add_convert_fusion.refs_1_, f32[64,256]{1,0:T(8,128)S(1)} %get-tuple-element.16.refs_2_, f32[1024,256]{1,0:T(8,128)S(1)} %get-tuple-element.17.refs_3_, ...), custom_call_target="tpu_custom_call" | custom-call | tf_op jit(solution)/shard_map/step/pallas_call | solution.py:343
  60.9 2.0 %all-gather.1 = bf16[34,32,128]{2,1,0:T(8,128)(2,1)S(1)} all-gather(bf16[17,32,128]{2,1,0:T(8,128)(2,1)S(1)} %get-tuple-element.24), channel_id=3, replica_groups=mesh['yhi'=2,'z'=8,'ylo'=4,'x'=4,'core'=2] {'core'}, dimensions={0}, use_global_device_ids=true | all-gather | bytes 417792 | tf_op jit(solution)/shard_map/all_gather | solution.py:121
  62.9 0.9 join.3
  63.7 11.2 %all_to_all.22 = bf16[16,32,128]{2,1,0:T(8,128)(2,1)S(1)} all-to-all(bf16[16,32,128]{2,1,0:T(8,128)(2,1)S(1)} %get-tuple-element.26), channel_id=1, replica_groups=mesh['yhi'=2,'z'=8,'ylo'=4,'x'=4,'core'=2] {'x','ylo'}, dimensions={0} | all-to-all | bytes 262144 | tf_op jit(solution)/shard_map/all_to_all | solution.py:137
  75.0 16.2 %all_to_all.23 = bf16[16,32,128]{2,1,0:T(8,128)(2,1)S(1)} all-to-all(bf16[16,32,128]{2,1,0:T(8,128)(2,1)S(1)} %bitcast.20), channel_id=1, replica_groups=mesh['yhi'=2,'z'=8,'ylo'=4,'x'=4,'core'=2] {'yhi','z'}, dimensions={0} | all-to-all | bytes 262144 | tf_op jit(solution)/shard_map/all_to_all | solution.py:137
  91.2 0.6 bitcast_add_fusion
  (6 shorter events, 0.1 us)
Async XLA Ops:
  0.0 3.6 %copy-start.2 = (f32[128,32]{0,1:T(8,128)S(1)}, f32[128,32]{0,1:T(8,128)}, u32[]{:S(2)}) copy-start(f32[128,32]{0,1:T(8,128)} %param.6) | copy-start | bytes 49156
  0.0 14.5 %copy-start = (bf16[2,128,1024]{2,1,0:T(8,128)(2,1)S(1)}, bf16[2,128,1024]{2,1,0:T(8,128)(2,1)}, u32[]{:S(2)}) copy-start(bf16[2,128,1024]{2,1,0:T(8,128)(2,1)} %param.7) | copy-start | bytes 1572868
  1.7 16.1 %collective-permute-start.1 = (bf16[1024,1024]{1,0:T(8,128)(2,1)S(1)}, bf16[1024,1024]{1,0:T(8,128)(2,1)S(1)}, u32[]{:S(2)}, u32[]{:S(2)}) collective-permute-start(bf16[1024,1024]{1,0:T(8,128)(2,1)S(1)} %split.1), channel_id=1, source_target_pairs={{0,1},{1,0},{2,3},{3,2},{4,5},{5,4},{6,7},{7,6},{8,9},{9,8},{10,11... | collective-permute-start | bytes 6291464 | tf_op jit(solution)/shard_map/ppermute | solution.py:362
  3.6 14.1 %collective-permute-start = (f32[32,128]{1,0:T(8,128)S(1)}, f32[32,128]{1,0:T(8,128)S(1)}, u32[]{:S(2)}, u32[]{:S(2)}) collective-permute-start(f32[32,128]{1,0:T(8,128)S(1)} %bitcast.27), channel_id=1, source_target_pairs={{0,12},{1,13},{32,10},{33,11},{64,8},{65,9},{96,2},{97,3},{128,0},... | collective-permute-start | bytes 49160 | tf_op jit(solution)/shard_map/ppermute | solution.py:92
  17.7 0.8 copy-start.1
